TPU v7x, 512 devices: a whole 4x4x16 slice. The times are simulated.
512 devices in a mesh: expert: 32 (over z, core), tensor: 16 (over y, x).
Axes of the slice: x: 4, y: 4, z: 16, core: 2. Of those that a mesh axis runs over, the one named last changes fastest.
Arguments:
- hidden_in: bfloat16 [4096, 4096], P('expert', 'tensor'), may hold values from -92 to 92
- norm_gain: float32 [4096], P('tensor'), may hold values from 0.5 to 1.5
- expert_ids: int32 [4096, 8], P('expert'), may hold values from 0 to 63, all different within a row; in each aligned block of 128 rows (0 to 127, 128 to 255, ...) at most 24 rows name the same one
- route_weights: float32 [4096, 8], P('expert'), may hold values from 0.05 to 0.5
- w_gate: bfloat16 [64, 1536, 4096], P('expert', 'tensor'), may hold values from -0.09375 to 0.09375
- w_up: bfloat16 [64, 1536, 4096], P('expert', 'tensor'), may hold values from -0.09375 to 0.09375
- w_down: bfloat16 [64, 1536, 4096], P('expert', 'tensor'), may hold values from -0.15625 to 0.15625
Outputs:
- moe_out: bfloat16 [4096, 4096], P('expert', 'tensor')
Inputs may be any that keep to these rules, and one draw needn't show every extreme that they name: `expert_ids`: in each aligned block of 128 rows (the rows of one index of the expert axis) no expert is named by more than 24 rows, a bound that some block reaches.
All inputs are finite; a program needn't handle non-finite values.
Results may differ from a plain program's by a relative error of at most 0.019.
Values may be sent and summed in bfloat16 or wider, within the bound.
A program may use at most 128 MiB of HBM per device.

v0:
```python
import jax
import jax.numpy as jnp
from jax import lax
from jax.sharding import PartitionSpec as P

D = 4096


epsilon = 1e-06


def local_partials(inner, w_down):
    partial_list = []
    for expert_slot in range(inner.shape[0]):
        partial_one = jnp.dot(
            inner[expert_slot], w_down[expert_slot], preferred_element_type=jnp.float32
        )
        partial_list.append(partial_one.astype(jnp.bfloat16))
    return jnp.stack(partial_list, axis=0)


def body(hidden_in, norm_gain, expert_ids, route_weights, w_gate, w_up, w_down):
    tokens_here = hidden_in.shape[0]
    width_local = hidden_in.shape[1]
    choices_count = expert_ids.shape[1]
    exp_local = w_gate.shape[0]
    groups = lax.axis_size("expert")
    experts_all = exp_local * groups
    capacity = min(tokens_here, 3 * tokens_here * choices_count // (2 * experts_all))
    widened = hidden_in.astype(jnp.float32)
    squares = lax.psum(jnp.sum(widened * widened, axis=1), "tensor")
    normed = (widened * lax.rsqrt(squares / D + epsilon)[:, None] * norm_gain[None, :]).astype(
        jnp.bfloat16
    )
    picked_mask = (
        expert_ids[:, :, None] == jnp.arange(experts_all, dtype=jnp.int32)[None, None, :]
    ).astype(jnp.int32)
    chosen = jnp.sum(picked_mask, axis=1)
    before = jnp.cumsum(chosen, axis=0) - chosen
    position = jnp.sum(picked_mask * before[:, None, :], axis=2)
    flat_index = expert_ids * capacity + position
    slot_ids = jnp.arange(experts_all * capacity, dtype=jnp.int32)
    placing = jnp.sum(
        (flat_index[None, :, :] == slot_ids[:, None, None]).astype(jnp.float32), axis=2
    ).astype(jnp.bfloat16)
    outgoing = jnp.dot(placing, normed, preferred_element_type=jnp.float32).astype(jnp.bfloat16)
    outgoing = outgoing.reshape(experts_all, capacity, width_local)
    arrived = lax.all_to_all(outgoing, "expert", split_axis=0, concat_axis=1, tiled=True)
    piece = lax.all_gather(arrived, "tensor", axis=2, tiled=True)
    gate_add = jnp.einsum("erd,efd->erf", piece, w_gate, preferred_element_type=jnp.float32)
    up_add = jnp.einsum("erd,efd->erf", piece, w_up, preferred_element_type=jnp.float32)
    inner = (jax.nn.silu(gate_add) * up_add).astype(jnp.bfloat16)
    partials = local_partials(inner, w_down)
    returned = lax.all_to_all(partials, "expert", split_axis=1, concat_axis=0, tiled=True)
    lookup = returned.reshape(experts_all * capacity, returned.shape[2])
    gathered = lookup[flat_index].astype(jnp.float32)
    weighted = jnp.sum(gathered * route_weights[:, :, None], axis=1)
    mixed = lax.psum_scatter(
        weighted.astype(jnp.bfloat16), "tensor", scatter_dimension=1, tiled=True
    )
    return mixed


def solution(mesh):
    placed = (
        P("expert", "tensor"),
        P("tensor"),
        P("expert", None),
        P("expert", None),
        P("expert", "tensor", None),
        P("expert", "tensor", None),
        P("expert", "tensor", None),
    )
    return jax.shard_map(
        body, mesh=mesh, in_specs=placed, out_specs=P("expert", "tensor"), check_vma=False
    )
```

profile of v0, /device:TPU:6, one launch (start us, length us, event | category | flops | bytes accessed | tf_op | source)
XLA Modules:
  0.0 977.3 jit_solution(5443993233181288136)
XLA Ops:
  6.5 0.0 copy-start
  6.5 0.0 all-gather.2.cloned.1.call-start
  6.5 0.8 convert_reduce_fusion.1
  7.4 0.1 copy.26
  7.5 0.2 reduce_window_sum.11
  7.7 0.1 copy.28
  7.7 0.7 select_reduce_fusion
  8.5 0.7 compare_select_fusion
  9.2 8.0 convert_reduce_fusion
  17.2 0.9 fusion.9
  18.2 37.4 %psum.7 = f32[128]{0:T(128)S(1)} all-reduce(f32[128]{0:T(128)S(1)} %fusion.9), channel_id=1, replica_groups=mesh['expert'=32,'tensor'=16] {'tensor'}, use_global_device_ids=true, to_apply=%region_5.6 | all-reduce | flops 128 | bytes 1024 | tf_op jit(solution)/shard_map/psum | solution.py:31
  55.5 1.3 convolution_convert_fusion.2
  56.8 55.5 %all_to_all.33 = bf16[64,24,256]{2,1,0:T(8,128)(2,1)S(1)} all-to-all(bf16[64,24,256]{2,1,0:T(8,128)(2,1)S(1)} %bitcast.36), channel_id=1, replica_groups=mesh['expert'=32,'tensor'=16] {'expert'}, dimensions={0} | all-to-all | bytes 1572864 | tf_op jit(solution)/shard_map/all_to_all | solution.py:48
  112.3 1.0 copy.29
  113.3 0.0 all-gather.2.cloned.1.call-update
  113.3 109.3 %all-gather.2.cloned.1.call-done = bf16[2,768,4096]{2,1,0:T(8,128)(2,1)} async-done(((bf16[2,768,256]{2,1,0:T(8,128)(2,1)}), bf16[2,768,4096]{2,1,0:T(8,128)(2,1)}) %all-gather.2.cloned.1.call-update) | async-done | bytes 12582928 | tf_op jit(solution)/shard_map/all_gather | solution.py:49
  222.6 0.0 copy-done
  222.6 8.5 fusion.15
  231.2 9.0 fusion.3
  240.2 3.0 fusion.1
  243.1 2.9 fusion.2
  246.1 1.2 pad_maximum_fusion
  247.3 33.0 %copy.30 = bf16[2,768,4096]{2,0,1:T(2,128)(2,1)} copy(bf16[2,768,4096]{2,1,0:T(8,128)(2,1)S(1)} %pad_maximum_fusion) | data formatting | bytes 25165824 | tf_op jit(solution)/shard_map/stack | solution.py:19
  280.4 0.0 copy-start.2
  280.4 12.8 %all-to-all-start.1 = ((bf16[2,768,4096]{2,0,1:T(2,128)(2,1)}), bf16[2,768,4096]{2,0,1:T(2,128)(2,1)}, u32[]{:S(2)}, u32[]{:S(2)}) async-start(bf16[2,768,4096]{2,0,1:T(2,128)(2,1)} %copy.30), calls=%async_computation.1 | async-start | bytes 25165824 | tf_op jit(solution)/shard_map/all_to_all | solution.py:54
  293.2 0.3 reduce-scatter.2.cloned.1.call-start
  293.5 0.1 copy.32
  293.6 0.1 reshape.25
  293.7 0.0 copy-done.2
  293.7 0.1 copy.33
  293.8 538.0 %all-to-all-done.1 = bf16[2,768,4096]{2,0,1:T(2,128)(2,1)} async-done(((bf16[2,768,4096]{2,0,1:T(2,128)(2,1)}), bf16[2,768,4096]{2,0,1:T(2,128)(2,1)}, u32[]{:S(2)}, u32[]{:S(2)}) %all-to-all-start.1) | async-done | bytes 12582944 | tf_op jit(solution)/shard_map/all_to_all | solution.py:54
  831.8 14.5 %copy.31 = bf16[2,32,24,4096]{3,2,0,1:T(8,128)(2,1)} copy(bf16[2,32,24,4096]{3,0,2,1:T(2,128)(2,1)} %bitcast.10) | data formatting | bytes 25165824 | tf_op jit(solution)/shard_map/all_to_all | solution.py:54
  846.3 0.0 copy-start.1
  846.3 21.4 %gather_fusion = bf16[1024,4096]{1,0:T(8,128)(2,1)} fusion(bf16[1536,4096]{1,0:T(8,128)(2,1)} %bitcast.33, s32[1024]{0:T(1024)S(1)} %broadcast_clamp_fusion), kind=kCustom, calls=%fused_computation | custom fusion | bytes 16781312 | tf_op jit(solution)/shard_map/gather | solution.py:56
  867.6 13.0 %fusion = bf16[128,4096]{1,0:T(8,128)(2,1)} fusion(bf16[1024,4096]{1,0:T(8,128)(2,1)} %gather_fusion, f32[128,8]{1,0:T(8,128)S(1)} %copy.33), kind=kLoop, calls=%fused_computation.2 | loop fusion | flops 12058624 | bytes 9441280 | tf_op jit(solution)/shard_map/reduce_sum | solution.py:57
  880.6 0.0 reduce-scatter.2.cloned.1.call-update
  880.7 89.8 %reduce-scatter.2.cloned.1.call-done = bf16[128,256]{1,0:T(8,128)(2,1)} async-done(((bf16[128,4096]{1,0:T(8,128)(2,1)}), bf16[128,256]{1,0:T(8,128)(2,1)}) %reduce-scatter.2.cloned.1.call-update) | async-done | bytes 65552 | tf_op jit(solution)/shard_map/reduce_scatter | solution.py:58
  970.4 0.0 copy-done.1
  (3 shorter events, 0.0 us)
Async XLA Ops:
  6.5 216.1 %copy-start = (bf16[2,96,4096]{2,1,0:T(8,128)(2,1)S(1)}, bf16[2,96,4096]{2,1,0:T(8,128)(2,1)}, u32[]{:S(2)}) copy-start(bf16[2,96,4096]{2,1,0:T(8,128)(2,1)} %param.11) | copy-start | bytes 4718596
  6.5 216.1 %all-gather.2.cloned.1.call-start = ((), (), s32[]{:S(2)}) async-start(), calls=%async_computation.3 | async-start | bytes 13369344 | tf_op jit(solution)/shard_map/all_gather | solution.py:49
  280.4 13.3 %copy-start.2 = (f32[128,8]{0,1:T(8,128)S(1)}, f32[128,8]{0,1:T(8,128)}, u32[]{:S(2)}) copy-start(f32[128,8]{0,1:T(8,128)} %param.10) | copy-start | bytes 12292
  280.4 551.4 %all-to-all-start.1 = ((bf16[2,768,4096]{2,0,1:T(2,128)(2,1)}), bf16[2,768,4096]{2,0,1:T(2,128)(2,1)}, u32[]{:S(2)}, u32[]{:S(2)}) async-start(bf16[2,768,4096]{2,0,1:T(2,128)(2,1)} %copy.30), calls=%async_computation.1 | async-start | bytes 25165824 | tf_op jit(solution)/shard_map/all_to_all | solution.py:54
  293.2 677.2 %reduce-scatter.2.cloned.1.call-start = ((), (), s32[]{:S(2)}) async-start(), calls=%async_computation.4 | async-start | bytes 1114112 | tf_op jit(solution)/shard_map/reduce_scatter | solution.py:58
  846.3 124.2 %copy-start.1 = (bf16[2,96,4096]{2,1,0:T(8,128)(2,1)S(1)}, bf16[2,96,4096]{2,1,0:T(8,128)(2,1)}, u32[]{:S(2)}) copy-start(bf16[2,96,4096]{2,1,0:T(8,128)(2,1)} %param.11) | copy-start | bytes 4718596
Sparse Core Ops, SparseCore 0:
  113.5 109.1 all-gather.1
  880.8 89.5 reduce-scatter.1
where the time goes:
time: 978 us; the launch traced here: 977 us
  waiting for transfers between devices  737 us (75%)
  blocking collectives  92.9 us (9%)
  local copies, waits for them, and re-layouts  70.4 us (7%)
  other arithmetic  25.7 us (3%)
  matrix products  24.7 us (3%)
  between operations  13.5 us (1%)
  starting transfers between devices  13.1 us (1%)
    all_to_all x1, waiting for transfers between devices, body(): lax.all_to_all(partials, 'expert', split_axis=1, concat_axis=0, tiled=True)  538 us
    all_gather x1, waiting for transfers between devices, body(): piece = lax.all_gather(arrived, 'tensor', axis=2, tiled=True)  109 us
    reduce_scatter x1, waiting for transfers between devices, body(): lax.psum_scatter(weighted.astype(jnp.bfloat16), 'tensor', scatter_dimensi...  89.8 us
    all_to_all x1, blocking collectives, body(): lax.all_to_all(outgoing, 'expert', split_axis=0, concat_axis=1, tiled=True)  55.5 us
    psum x1, blocking collectives, body(): squares = lax.psum(jnp.sum(widened * widened, axis=1), 'tensor')  37.4 us
    another operation x1, local copies, waits for them, and re-layouts, local_partials(): return jnp.stack(partial_list, axis=0)  33 us
    gather x1, local copies, waits for them, and re-layouts, body(): gathered = lookup[flat_index].astype(jnp.float32)  21.4 us
  transfers between devices with their start and end apart: 3, of which 3 were waited for; matrix products, arithmetic and copies ran while one was open for 0% of the time, Pallas kernels for 0%

commit v1 on v0

v1 whole, which is shorter than its diff:
```python
import jax
import jax.numpy as jnp
from jax import lax
from jax.sharding import PartitionSpec as P

D = 4096


epsilon = 1e-06


def body(hidden_in, norm_gain, expert_ids, route_weights, w_gate, w_up, w_down):
    tokens_here = hidden_in.shape[0]
    choices_count = expert_ids.shape[1]
    exp_local = w_gate.shape[0]
    groups = lax.axis_size("expert")
    experts_all = exp_local * groups
    capacity = min(tokens_here, 3 * tokens_here * choices_count // (2 * experts_all))
    widened = hidden_in.astype(jnp.float32)
    squares = lax.psum(jnp.sum(widened * widened, axis=1), "tensor")
    normed = (widened * lax.rsqrt(squares / D + epsilon)[:, None] * norm_gain[None, :]).astype(
        jnp.bfloat16
    )
    routing = jnp.concatenate([expert_ids.astype(jnp.float32), route_weights], axis=1)
    routing = lax.all_gather(routing.T, "expert", axis=0, tiled=False)
    tokens_all = lax.all_gather(normed, "expert", axis=0, tiled=False)
    first = (lax.axis_index("expert") * exp_local).astype(jnp.float32)
    named = routing[:, None, :choices_count, :] == (
        first + jnp.arange(exp_local, dtype=jnp.float32)[None, :, None, None]
    )
    chosen = jnp.any(named, axis=2)
    scale = jnp.sum(jnp.where(named, routing[:, None, choices_count:, :], 0.0), axis=2)
    step = jnp.arange(tokens_here, dtype=jnp.int32)
    earlier = (step[:, None] < step[None, :]).astype(jnp.bfloat16)
    position = jnp.einsum(
        "bjs,st->bjt", chosen.astype(jnp.bfloat16), earlier, preferred_element_type=jnp.float32
    )
    slot = jnp.arange(capacity, dtype=jnp.float32)
    select = (
        (position[:, :, None, :] == slot[None, None, :, None]) & chosen[:, :, None, :]
    ).astype(jnp.bfloat16)
    rows = jnp.einsum(
        "bjst,btd->bjsd", select, tokens_all, preferred_element_type=jnp.float32
    ).astype(jnp.bfloat16)
    rows = rows.transpose(1, 0, 2, 3).reshape(exp_local, groups * capacity, -1)
    piece = lax.all_gather(rows, "tensor", axis=2, tiled=True)
    gate_add = jnp.einsum("erd,efd->erf", piece, w_gate, preferred_element_type=jnp.float32)
    up_add = jnp.einsum("erd,efd->erf", piece, w_up, preferred_element_type=jnp.float32)
    inner = (jax.nn.silu(gate_add) * up_add).astype(jnp.bfloat16)
    partials = jnp.einsum(
        "erf,efd->erd", inner, w_down, preferred_element_type=jnp.float32
    ).astype(jnp.bfloat16)
    summed = lax.psum_scatter(partials, "tensor", scatter_dimension=2, tiled=True)
    summed = summed.reshape(exp_local, groups, capacity, -1)
    back = jnp.einsum(
        "bjst,jbsd->bjtd", select, summed, preferred_element_type=jnp.float32
    )
    weighted = jnp.sum(back * scale[:, :, :, None], axis=1).astype(jnp.bfloat16)
    return lax.psum_scatter(weighted, "expert", scatter_dimension=0, tiled=False)


def solution(mesh):
    placed = (
        P("expert", "tensor"),
        P("tensor"),
        P("expert", None),
        P("expert", None),
        P("expert", "tensor", None),
        P("expert", "tensor", None),
        P("expert", "tensor", None),
    )
    return jax.shard_map(
        body, mesh=mesh, in_specs=placed, out_specs=P("expert", "tensor"), check_vma=False
    )
```

time: 978 us -> 492 us (0.50)
  waiting for transfers between devices: 737 us -> 371 us
  local copies, waits for them, and re-layouts: 70.4 us -> 1.03 us
  blocking collectives: 92.9 us -> 69.7 us
  other arithmetic: 25.7 us -> 4.34 us
  starting transfers between devices: 13.1 us -> 0.13 us
    all_to_all x1 -> x0, waiting for transfers between devices: 538 us -> none  [body(): lax.all_to_all(partials, 'expert', split_axis=1, concat_axis=0, tiled=True)]
    reduce_scatter x1 -> x2, waiting for transfers between devices: 89.8 us -> 219 us  [the longest x1 110 us: body(): lax.psum_scatter(weighted, 'expert', scatter_dimension=0, tiled=False)]
    all_to_all x1 -> x0, blocking collectives: 55.5 us -> none  [body(): lax.all_to_all(outgoing, 'expert', split_axis=0, concat_axis=1, tiled=True)]
    all_gather x1 -> x2, waiting for transfers between devices: 109 us -> 152 us  [the longest x1 112 us: body(): piece = lax.all_gather(rows, 'tensor', axis=2, tiled=True)]
    another operation x1 -> x0, local copies, waits for them, and re-layouts: 33 us -> none  [local_partials(): return jnp.stack(partial_list, axis=0)]
    all_gather x0 -> x1, blocking collectives: none -> 32.3 us  [body(): routing = lax.all_gather(routing.T, 'expert', axis=0, tiled=False)]
    reduce_sum x4 -> x1, other arithmetic: 22.6 us -> 0.17 us  [body(): jnp.sum(jnp.where(named, routing[:, None, choices_count:, :], 0.0), axis=2)]
    gather x1 -> x0, local copies, waits for them, and re-layouts: 21.4 us -> none  [body(): gathered = lookup[flat_index].astype(jnp.float32)]
  transfers between devices with their start and end apart: 3 -> 4, of which waited for: 3 -> 4; matrix products, arithmetic and copies ran while one was open for 0% -> 0% of each run, Pallas kernels for 0% -> 0%
where the time goes in v1:
time: 492 us; the launch traced here: 491 us
  waiting for transfers between devices  371 us (75%)
  blocking collectives  69.7 us (14%)
  matrix products  31.7 us (6%)
  between operations  13.2 us (3%)
    all_gather x1, waiting for transfers between devices, body(): piece = lax.all_gather(rows, 'tensor', axis=2, tiled=True)  112 us
    reduce_scatter x1, waiting for transfers between devices, body(): lax.psum_scatter(weighted, 'expert', scatter_dimension=0, tiled=False)  110 us
    reduce_scatter x1, waiting for transfers between devices, body(): lax.psum_scatter(partials, 'tensor', scatter_dimension=2, tiled=True)  109 us
    all_gather x1, waiting for transfers between devices, body(): tokens_all = lax.all_gather(normed, 'expert', axis=0, tiled=False)  40.4 us
    psum x1, blocking collectives, body(): squares = lax.psum(jnp.sum(widened * widened, axis=1), 'tensor')  37.4 us
    all_gather x1, blocking collectives, body(): routing = lax.all_gather(routing.T, 'expert', axis=0, tiled=False)  32.3 us
    dot_general x1, matrix products, body(): jnp.einsum('erf,efd->erd', inner, w_down, preferred_element_type=jnp.floa...  15.3 us
  transfers between devices with their start and end apart: 4, of which 4 were waited for; matrix products, arithmetic and copies ran while one was open for 0% of the time, Pallas kernels for 0%

profile of v1, /device:TPU:6, one launch (start us, length us, event | category | flops | bytes accessed | tf_op | source)
XLA Modules:
  0.0 491.0 jit_solution(8719006843433217021)
XLA Ops:
  6.5 0.0 copy-start
  6.5 0.0 all-gather.7.cloned.1.call-start
  6.5 1.1 fusion.17
  7.6 37.4 %psum.7 = f32[128]{0:T(128)S(1)} all-reduce(f32[128]{0:T(128)S(1)} %fusion.17), channel_id=1, replica_groups=mesh['expert'=32,'tensor'=16] {'tensor'}, use_global_device_ids=true, to_apply=%region_2.0 | all-reduce | flops 128 | bytes 1024 | tf_op jit(solution)/shard_map/psum | solution.py:20
  45.0 1.6 fusion.19
  46.5 0.0 all-gather.7.cloned.1.call-update
  46.6 0.0 all-gather.5.cloned.1.call-start
  46.6 0.7 convert_element_type.31
  47.3 0.7 maximum_bitcast_fusion
  48.0 32.3 %all-gather = f32[512,128]{1,0:T(8,128)S(1)} all-gather(f32[16,128]{1,0:T(8,128)S(1)} %maximum_bitcast_fusion), channel_id=2, replica_groups=mesh['expert'=32,'tensor'=16] {'expert'}, dimensions={0}, use_global_device_ids=true | all-gather | bytes 270336 | tf_op jit(solution)/shard_map/all_gather | solution.py:25
  80.4 0.2 compare_reduce_fusion
  80.5 0.1 fusion.21
  80.7 40.4 %all-gather.7.cloned.1.call-done = bf16[4096,256]{1,0:T(8,128)(2,1)} async-done(((bf16[128,256]{1,0:T(8,128)(2,1)}), bf16[4096,256]{1,0:T(8,128)(2,1)}) %all-gather.7.cloned.1.call-update) | async-done | bytes 2097168 | tf_op jit(solution)/shard_map/all_gather | solution.py:26
  121.1 2.0 fusion
  123.1 1.0 copy.17
  124.1 0.0 all-gather.5.cloned.1.call-update
  124.1 0.0 reduce-scatter.3.cloned.1.call-start
  124.2 111.9 %all-gather.5.cloned.1.call-done = bf16[2,768,4096]{2,1,0:T(8,128)(2,1)} async-done(((bf16[2,768,256]{2,1,0:T(8,128)(2,1)}), bf16[2,768,4096]{2,1,0:T(8,128)(2,1)}) %all-gather.5.cloned.1.call-update) | async-done | bytes 12582928 | tf_op jit(solution)/shard_map/all_gather | solution.py:46
  236.1 9.0 %fusion.26 = f32[2,768,96]{1,2,0:T(8,128)S(1)} fusion(bf16[2,768,4096]{2,1,0:T(8,128)(2,1)} %all-gather.5.cloned.1.call-done, bf16[2,96,4096]{2,1,0:T(8,128)(2,1)} %param.11), kind=kOutput, calls=%fused_computation.36 | convolution fusion | flops 1207959552 | bytes 14745600 | tf_op jit(solution)/shard_map/erd,efd->erf/dot_general | solution.py:47
  245.0 0.0 copy-done
  245.1 15.3 %convolution_convert_fusion = bf16[2,768,4096]{2,1,0:T(8,128)(2,1)} fusion(bf16[2,96,4096]{2,1,0:T(8,128)(2,1)S(1)} %copy-done, bf16[2,768,4096]{2,1,0:T(8,128)(2,1)} %all-gather.5.cloned.1.call-done, bf16[2,96,4096]{2,1,0:T(8,128)(2,1)} %param.12, f32[2,768,96]{1,2,0:T(8,128)S(1)} %fusion.26), kind=kOutput, calls=%fused_computation | convolution fusion | flops 2423095296 | bytes 28901376 | tf_op jit(solution)/shard_map/erf,efd->erd/dot_general | solution.py:50
  260.4 0.0 reduce-scatter.3.cloned.1.call-update
  260.4 0.0 reduce-scatter.5.cloned.1.call-start
  260.4 0.2 fusion.16
  260.6 109.0 %reduce-scatter.3.cloned.1.call-done = bf16[2,768,256]{2,1,0:T(8,128)(2,1)} async-done(((bf16[2,768,4096]{2,1,0:T(8,128)(2,1)}), bf16[2,768,256]{2,1,0:T(8,128)(2,1)}) %reduce-scatter.3.cloned.1.call-update) | async-done | bytes 786448 | tf_op jit(solution)/shard_map/reduce_scatter | solution.py:53
  369.6 5.3 %multiply_reduce_fusion = bf16[32,128,256]{2,1,0:T(8,128)(2,1)} fusion(f32[32,2,128]{2,1,0:T(2,128)S(1)} %fusion.16, bf16[2,32,24,256]{3,2,1,0:T(8,128)(2,1)} %bitcast.25, f32[32,2,128]{2,1,0:T(2,128)S(1)} %copy.16, pred[32,2,128]{2,1,0:T(4,128)(4,1)S(1)} %compare_reduce_fusion), kind=kOutput, calls=%fused_computation.1 | convolution fusion | flops 104202240 | bytes 2957312 | tf_op jit(solution)/shard_map/bjst,jbsd->bjtd/dot_general | solution.py:55
  374.9 0.0 reduce-scatter.5.cloned.1.call-update
  374.9 109.6 %reduce-scatter.5.cloned.1.call-done = bf16[1,128,256]{2,1,0:T(8,128)(2,1)} async-done(((bf16[32,128,256]{2,1,0:T(8,128)(2,1)}), bf16[1,128,256]{2,1,0:T(8,128)(2,1)}) %reduce-scatter.5.cloned.1.call-update) | async-done | bytes 65552 | tf_op jit(solution)/shard_map/reduce_scatter | solution.py:59
  (4 shorter events, 0.1 us)
Async XLA Ops:
  6.5 238.5 %copy-start = (bf16[2,96,4096]{2,1,0:T(8,128)(2,1)S(1)}, bf16[2,96,4096]{2,1,0:T(8,128)(2,1)}, u32[]{:S(2)}) copy-start(bf16[2,96,4096]{2,1,0:T(8,128)(2,1)} %param.13) | copy-start | bytes 4718596
  6.5 114.6 %all-gather.7.cloned.1.call-start = ((), (), s32[]{:S(2)}) async-start(), calls=%async_computation.5 | async-start | bytes 2162688 | tf_op jit(solution)/shard_map/all_gather | solution.py:26
  46.6 189.5 %all-gather.5.cloned.1.call-start = ((), (), s32[]{:S(2)}) async-start(), calls=%async_computation.2 | async-start | bytes 13369344 | tf_op jit(solution)/shard_map/all_gather | solution.py:46
  124.1 245.5 %reduce-scatter.3.cloned.1.call-start = ((), (), s32[]{:S(2)}) async-start(), calls=%async_computation.3 | async-start | bytes 13369344 | tf_op jit(solution)/shard_map/reduce_scatter | solution.py:53
  260.4 224.1 %reduce-scatter.5.cloned.1.call-start = ((), (), s32[]{:S(2)}) async-start(), calls=%async_computation.4 | async-start | bytes 2162688 | tf_op jit(solution)/shard_map/reduce_scatter | solution.py:59
Sparse Core Ops, SparseCore 0:
  46.7 74.3 all-gather.6
  124.3 111.7 all-gather.4
  260.5 109.0 reduce-scatter.2
  375.1 109.3 reduce-scatter.4

commit v2 on v1

v2 whole, which is shorter than its diff:
```python
import functools

import jax
import jax.numpy as jnp
from jax import lax
from jax.experimental import pallas as pl
from jax.experimental.pallas import tpu as pltpu
from jax.sharding import PartitionSpec as P

epsilon = 1e-06
SIDE = 4
BF = jnp.bfloat16
F32 = jnp.float32


def dot(a, b, ca, cb):
    return lax.dot_general(a, b, (((ca,), (cb,)), ((), ())), preferred_element_type=F32)


def kernel(
    Z, capacity, width,
    hid, gain, route, w_gate, w_up, w_down, out,
    tok, rows, gath, wts, accg, accu, inner, part, hop, from_l, from_r, vsum, cross, final,
    sw, cont, sib, zin, sqb,
    sq_s, sq_r, za_s, za_r, sb_s, sb_r, wl_r, w_s, w_r, a_s, a_r, b_s, b_r, f_s, f_r,
    r1_s, r1_r, r2_s, r2_r, c_s, c_r, cs_s, cs_r, q_s, q_r,
):
    H = Z // 2
    A = H // 2
    n = hid.shape[0]
    wide = hid.shape[1]
    fh = w_gate.shape[1]
    topk = route.shape[0] // 2
    experts = 4 * Z
    two = 2 * capacity
    half_rows = H * two

    E = lax.axis_index("expert")
    T = lax.axis_index("tensor")
    z, c = lax.div(E, 2), lax.rem(E, 2)
    y, x = lax.div(T, SIDE), lax.rem(T, SIDE)

    def mod(v, m):
        return lax.rem(v + m, m)

    def axes(j):
        return (x + j * (y - x), y + j * (x - y))

    def device(j, a, b):
        return (E, (b + j * (a - b)) * SIDE + a + j * (b - a))

    def column(j, sh):
        bb, aa = lax.div(sh, SIDE), lax.rem(sh, SIDE)
        t = bb * SIDE + aa + j * (aa * SIDE + bb - bb * SIDE - aa)
        return pl.ds(pl.multiple_of(t * wide, wide), wide)

    def send(src, dst, ssem, rsem, to):
        pltpu.make_async_remote_copy(
            src_ref=src, dst_ref=dst, send_sem=ssem, recv_sem=rsem,
            device_id=to, device_id_type=pl.DeviceIdType.MESH,
        ).start()

    def got(dst, ssem, rsem):
        pltpu.make_async_remote_copy(
            src_ref=dst, dst_ref=dst, send_sem=ssem, recv_sem=rsem,
            device_id=(E, T), device_id_type=pl.DeviceIdType.MESH,
        ).wait_recv()

    def left(src, ssem, rsem):
        pltpu.make_async_remote_copy(
            src_ref=src, dst_ref=src, send_sem=ssem, recv_sem=rsem,
            device_id=(E, T), device_id_type=pl.DeviceIdType.MESH,
        ).wait_send()

    other = (2 * z + 1 - c, T)
    z_up = (2 * mod(z + 1, Z) + c, T)
    z_down = (2 * mod(z - 1, Z) + c, T)

    barrier = pltpu.get_barrier_semaphore()
    partners = [other, z_up, z_down]
    for m in range(1, SIDE):
        partners.append((E, y * SIDE + mod(x + m, SIDE)))
        partners.append((E, mod(y + m, SIDE) * SIDE + x))
    for partner in partners:
        pl.semaphore_signal(barrier, inc=1, device_id=partner, device_id_type=pl.DeviceIdType.MESH)
    pl.semaphore_wait(barrier, len(partners))

    xx = hid[...].astype(F32)
    sq = jnp.sum(xx * xx, axis=1, keepdims=True)
    sqb[0, 0] = jnp.broadcast_to(sq, (n, 128)).T[0:8, :]
    for ph in range(2):
        for m in range(1, SIDE):
            to = (
                (E, y * SIDE + mod(x - m, SIDE)) if ph == 0 else (E, mod(y - m, SIDE) * SIDE + x)
            )
            send(sqb.at[ph, 0], sqb.at[ph, m], sq_s.at[ph, m], sq_r.at[ph, m], to)
        if ph == 0:
            ids = route[0:topk, :]
            wts_t = route[topk : 2 * topk, :]
            e_iota = lax.broadcasted_iota(jnp.int32, (experts, n), 0).astype(F32)
            hits = [e_iota == ids[k : k + 1, :] for k in range(topk)]
            chosen = jnp.zeros((experts, n), F32)
            for k in range(topk):
                chosen = chosen + jnp.where(hits[k], 1.0, 0.0)
            tri = (
                lax.broadcasted_iota(jnp.int32, (n, n), 0)
                < lax.broadcasted_iota(jnp.int32, (n, n), 1)
            ).astype(F32).astype(BF)
            before = dot(chosen.astype(BF), tri, 1, 0)
            pos = jnp.concatenate(
                [
                    jnp.sum(jnp.where(hits[k], before, 0.0), axis=0, keepdims=True)
                    for k in range(topk)
                ],
                axis=0,
            )
            high = wts_t.astype(BF).astype(F32)
            low = wts_t - high
            meta = jnp.concatenate(
                [jnp.concatenate([ids, high], axis=1), jnp.concatenate([low, pos], axis=1)], axis=0
            )
            tok[E, n : n + 2 * topk, :] = meta.astype(BF)
        for m in range(1, SIDE):
            got(sqb.at[ph, m], sq_s.at[ph, m], sq_r.at[ph, m])
        total = sqb[ph, 0] + sqb[ph, 1] + sqb[ph, 2] + sqb[ph, 3]
        if ph == 0:
            sqb[1, 0] = total
    scale = lax.rsqrt(total / width + epsilon)
    scale = jnp.broadcast_to(scale[0:1, :], (128, n)).T[:, 0:1]
    tok[E, 0:n, :] = (xx * scale * gain[...]).astype(BF)

    send(tok.at[E], tok.at[E], za_s.at[0, 0], za_r.at[0, 0], z_up)
    send(tok.at[E], tok.at[E], za_s.at[1, 0], za_r.at[1, 0], z_down)
    send(tok.at[E], tok.at[E], sb_s.at[0], sb_r.at[0], other)

    for j in range(2):
        a, b = axes(j)
        up = lax.rem(a + c, 2)
        mate = mod(a + 1 - 2 * up, SIDE)
        for i, w in enumerate((w_gate, w_up, w_down)):
            pltpu.make_async_copy(w.at[j], wts.at[j, i, pl.ds(0, fh)], wl_r.at[j, i]).start()
            send(w.at[j], wts.at[j, i, pl.ds(fh, fh)], w_s.at[j, i], w_r.at[j, i], device(j, mate, b))

    r_iota = lax.broadcasted_iota(jnp.int32, (two, 2 * n), 0).astype(F32)
    lane = lax.broadcasted_iota(jnp.int32, (1, 2 * n), 1)
    shift = jnp.where(lane >= n, float(capacity), 0.0)
    mine = (2 * E).astype(F32)

    def select(p, order):
        got(tok.at[2 * p + 1 - c], sb_s.at[order], sb_r.at[order])
        m0 = tok[2 * p, n : n + 2 * topk, :].astype(F32)
        m1 = tok[2 * p + 1, n : n + 2 * topk, :].astype(F32)

        def both(r, l):
            return jnp.concatenate(
                [
                    m0[r * topk : (r + 1) * topk, l * n : (l + 1) * n],
                    m1[r * topk : (r + 1) * topk, l * n : (l + 1) * n],
                ],
                axis=1,
            )

        ids, high, low, pos = both(0, 0), both(0, 1), both(1, 0), both(1, 1)
        picked = []
        for j in range(2):
            hit = ids == mine + float(j)
            named = jnp.sum(jnp.where(hit, 1.0, 0.0), axis=0, keepdims=True)
            slot = jnp.sum(jnp.where(hit, pos, 0.0), axis=0, keepdims=True)
            wh = jnp.sum(jnp.where(hit, high, 0.0), axis=0, keepdims=True)
            wo = jnp.sum(jnp.where(hit, low, 0.0), axis=0, keepdims=True)
            slot = jnp.where(named > 0.5, slot + shift, -1.0)
            chosen = jnp.where(r_iota == slot, 1.0, 0.0)
            sw[p, j * two : (j + 1) * two, :] = (chosen * wh).astype(BF)
            sw[p, (2 + j) * two : (3 + j) * two, :] = (chosen * wo).astype(BF)
            picked.append(chosen.astype(BF))
        pair = tok[pl.ds(2 * p, 2), 0:n, :].reshape(2 * n, wide)
        taken = dot(jnp.concatenate(picked, axis=0), pair, 1, 0).astype(BF)
        rows[0, p] = taken[0:two, :]
        rows[1, p] = taken[two : 2 * two, :]

    def z_step(s, carry):
        pr, po = mod(z - 1 - s, Z), mod(z + 1 + s, Z)
        br, bo = tok.at[2 * pr + c], tok.at[2 * po + c]
        got(br, za_s.at[0, s], za_r.at[0, s])

        @pl.when(s < H - 1)
        def _():
            send(br, br, za_s.at[0, s + 1], za_r.at[0, s + 1], z_up)

        send(br, br, sb_s.at[1 + s], sb_r.at[1 + s], other)

        @pl.when(s < H - 1)
        def _():
            got(bo, za_s.at[1, s], za_r.at[1, s])

            @pl.when(s < H - 2)
            def _():
                send(bo, bo, za_s.at[1, s + 1], za_r.at[1, s + 1], z_down)

            send(bo, bo, sb_s.at[1 + H + s], sb_r.at[1 + H + s], other)

        select(mod(z - s, Z), s)

        @pl.when(s > 0)
        def _():
            select(mod(z + s, Z), H + s)

        return carry

    lax.fori_loop(0, H, z_step, 0)
    select(mod(z - H, Z), H)

    for j in range(2):
        a, b = axes(j)
        sh = b * SIDE + a
        pltpu.make_async_copy(
            rows.at[j, pl.ds(H * lax.rem(a, 2), H)], gath.at[j, sh], a_r.at[j, 0]
        ).start()
        for k in (1, 3, 2):
            to = mod(a - k, SIDE)
            send(
                rows.at[j, pl.ds(H * lax.rem(to, 2), H)], gath.at[j, sh],
                a_s.at[j, k], a_r.at[j, k], device(j, to, b),
            )
    accg[...] = jnp.zeros_like(accg)
    accu[...] = jnp.zeros_like(accu)
    for j in range(2):
        a, b = axes(j)
        pltpu.make_async_copy(
            rows.at[j, pl.ds(H * lax.rem(a, 2), H)], gath.at[j, b * SIDE + a], a_r.at[j, 0]
        ).wait()
        for i, w in enumerate((w_gate, w_up, w_down)):
            pltpu.make_async_copy(w.at[j], wts.at[j, i, pl.ds(0, fh)], wl_r.at[j, i]).wait()

    def forward_own(j, k):
        a, b = axes(j)
        sh = b * SIDE + mod(a + k, SIDE)
        piece = gath.at[j, sh]
        send(piece, piece, b_s.at[j, k, 0], b_r.at[j, k, 0], device(j, a, mod(b + 1, SIDE)))
        send(piece, piece, b_s.at[j, k, 1], b_r.at[j, k, 1], device(j, a, mod(b - 1, SIDE)))

    for j in range(2):
        forward_own(j, 0)
    for j in range(2):
        for i in range(3):
            got(wts.at[j, i, pl.ds(fh, fh)], w_s.at[j, i], w_r.at[j, i])

    def multiply(j, sh):
        piece = gath[j, sh].reshape(half_rows, wide)
        col = column(j, sh)
        accg[j] += dot(piece, wts[j, 0, :, col], 1, 1)
        accu[j] += dot(piece, wts[j, 1, :, col], 1, 1)

    def gather_near(i, carry):
        j, k = lax.rem(i, 2), lax.div(i, 2)
        a, b = axes(j)
        sh = b * SIDE + mod(a + k, SIDE)

        @pl.when(k > 0)
        def _():
            got(gath.at[j, sh], a_s.at[j, k], a_r.at[j, k])
            forward_own(j, k)

        multiply(j, sh)
        return carry

    lax.fori_loop(0, 2 * SIDE, gather_near, 0)

    def gather_side(i, carry):
        j, k = lax.rem(i, 2), lax.div(i, 2)
        a, b = axes(j)
        low = mod(b - 1, SIDE) * SIDE + mod(a + k, SIDE)
        high = mod(b + 1, SIDE) * SIDE + mod(a + k, SIDE)
        got(gath.at[j, low], b_s.at[j, k, 0], b_r.at[j, k, 0])

        @pl.when(lax.rem(k, 2) == 0)
        def _():
            piece = gath.at[j, low]
            send(piece, piece, f_s.at[j, k], f_r.at[j, k], device(j, a, mod(b + 1, SIDE)))

        got(gath.at[j, high], b_s.at[j, k, 1], b_r.at[j, k, 1])

        @pl.when(lax.rem(k, 2) == 1)
        def _():
            piece = gath.at[j, high]
            send(piece, piece, f_s.at[j, k], f_r.at[j, k], device(j, a, mod(b - 1, SIDE)))

        multiply(j, low)
        multiply(j, high)
        return carry

    lax.fori_loop(0, 2 * SIDE, gather_side, 0)

    def gather_far(i, carry):
        j, k = lax.rem(i, 2), lax.div(i, 2)
        a, b = axes(j)
        sh = mod(b + 2, SIDE) * SIDE + mod(a + k, SIDE)
        got(gath.at[j, sh], f_s.at[j, k], f_r.at[j, k])
        multiply(j, sh)
        return carry

    lax.fori_loop(0, 2 * SIDE, gather_far, 0)

    for j in range(2):
        g = accg[j]
        inner[j] = (g / (1.0 + jnp.exp(-g)) * accu[j]).astype(BF)

    for d in (2, 1, 3, 0):
        for j in range(2):
            a, b = axes(j)
            first = mod(b + d, SIDE) * SIDE

            def down(aa, carry, j=j, first=first):
                sh = first + aa
                made = dot(inner[j], wts[j, 2, :, column(j, sh)], 1, 0).astype(BF)
                part[j, sh] = made.reshape(H, two, wide)
                return carry

            lax.fori_loop(0, SIDE, down, 0)
            bundle = part.at[j, pl.ds(first, SIDE)]
            above, below = device(j, a, mod(b + 1, SIDE)), device(j, a, mod(b - 1, SIDE))
            lo, hi = pl.ds(0, A), pl.ds(A, A)
            if d == 2:
                send(bundle.at[:, lo], hop.at[j, 0], r1_s.at[j, 0], r1_r.at[j, 0], above)
                send(bundle.at[:, hi], hop.at[j, 1], r1_s.at[j, 1], r1_r.at[j, 1], below)
            elif d == 1:
                send(bundle.at[:, hi], from_l.at[j, :, hi], r1_s.at[j, 2], r1_r.at[j, 2], above)
            elif d == 3:
                send(bundle.at[:, lo], from_r.at[j, :, lo], r1_s.at[j, 3], r1_r.at[j, 3], below)

    lo, hi = pl.ds(0, A), pl.ds(A, A)
    for j in range(2):
        a, b = axes(j)
        above, below = device(j, a, mod(b + 1, SIDE)), device(j, a, mod(b - 1, SIDE))
        for side, (d, cut, target, to) in enumerate(
            ((1, lo, from_l, above), (3, hi, from_r, below))
        ):
            first = mod(b + d, SIDE) * SIDE
            got(hop.at[j, side], r1_s.at[j, side], r1_r.at[j, side])

            def add_hop(aa, carry, j=j, first=first, cut=cut, side=side):
                mixed = part[j, first + aa, cut].astype(F32) + hop[j, side, aa].astype(F32)
                part[j, first + aa, cut] = mixed.astype(BF)
                return carry

            lax.fori_loop(0, SIDE, add_hop, 0)
            send(
                part.at[j, pl.ds(first, SIDE), cut], target.at[j, :, cut],
                r2_s.at[j, side], r2_r.at[j, side], to,
            )

    for j in range(2):
        a, b = axes(j)
        got(from_l.at[j, :, hi], r1_s.at[j, 2], r1_r.at[j, 2])
        got(from_r.at[j, :, lo], r1_s.at[j, 3], r1_r.at[j, 3])
        got(from_l.at[j, :, lo], r2_s.at[j, 0], r2_r.at[j, 0])
        got(from_r.at[j, :, hi], r2_s.at[j, 1], r2_r.at[j, 1])
        for m in (2, 1, 3, 0):
            aa = mod(a + m, SIDE)
            mixed = (
                part[j, b * SIDE + aa].astype(F32)
                + from_l[j, aa].astype(F32)
                + from_r[j, aa].astype(F32)
            )
            vsum[j, m] = mixed.astype(BF)
            if m:
                send(vsum.at[j, m], cross.at[j, m], c_s.at[j, m], c_r.at[j, m], device(j, aa, b))
    for j in range(2):
        a, b = axes(j)
        own = lax.rem(a, 2)
        for m in (1, 3, 2):
            got(cross.at[j, m], c_s.at[j, m], c_r.at[j, m])
        final[j, pl.ds(H * (1 - own), H)] = (
            cross[j, 1].astype(F32) + cross[j, 3].astype(F32)
        ).astype(BF)
        final[j, pl.ds(H * own, H)] = (vsum[j, 0].astype(F32) + cross[j, 2].astype(F32)).astype(BF)

    def combine(p):
        stacked = jnp.concatenate([final[0, p], final[1, p]], axis=0)
        stacked = jnp.concatenate([stacked, stacked], axis=0)
        made = dot(sw[p], stacked, 0, 0).astype(BF)
        cont[p, 0] = made[0:n, :]
        cont[p, 1] = made[n : 2 * n, :]
        send(cont.at[p, 1 - c], sib.at[p], cs_s.at[p], cs_r.at[p], other)

    hn = n // 2

    def spots(s):
        return mod(z + H - s, Z), mod(z + H + 1 + s, Z)

    for p in spots(0):
        combine(p)

    def ring(s, carry):
        p1, p2 = spots(s)

        @pl.when(s < H - 1)
        def _():
            for p in spots(s + 1):
                combine(p)

        for way, p, to in ((0, p1, z_up), (1, p2, z_down)):
            got(sib.at[p], cs_s.at[p], cs_r.at[p])

            for u in range(2):
                cut = pl.ds(u * hn, hn)

                @pl.when(s == 0)
                def _():
                    cont[p, c, cut] = (
                        cont[p, c, cut].astype(F32) + sib[p, cut].astype(F32)
                    ).astype(BF)

                @pl.when(s > 0)
                def _():
                    got(zin.at[way, s - 1, cut], q_s.at[way, s - 1, u], q_r.at[way, s - 1, u])
                    cont[p, c, cut] = (
                        cont[p, c, cut].astype(F32)
                        + sib[p, cut].astype(F32)
                        + zin[way, s - 1, cut].astype(F32)
                    ).astype(BF)

                @pl.when(s + way < H)
                def _():
                    send(
                        cont.at[p, c, cut], zin.at[way, s, cut],
                        q_s.at[way, s, u], q_r.at[way, s, u], to,
                    )

        return carry

    lax.fori_loop(0, H, ring, 0)
    for u in range(2):
        cut = pl.ds(u * hn, hn)
        got(zin.at[0, H - 1, cut], q_s.at[0, H - 1, u], q_r.at[0, H - 1, u])
        out[cut] = (cont[z, c, cut].astype(F32) + zin[0, H - 1, cut].astype(F32)).astype(BF)

    for ph in range(2):
        for m in range(1, SIDE):
            left(sqb.at[ph, 0], sq_s.at[ph, m], sq_r.at[ph, m])

    def left_z(s, carry):
        left(tok.at[0], za_s.at[0, s], za_r.at[0, s])

        @pl.when(s < H - 1)
        def _():
            left(tok.at[0], za_s.at[1, s], za_r.at[1, s])

        for u in range(2):
            cut = pl.ds(u * hn, hn)
            left(zin.at[0, 0, cut], q_s.at[0, s, u], q_r.at[0, s, u])

            @pl.when(s < H - 1)
            def _():
                left(zin.at[1, 0, cut], q_s.at[1, s, u], q_r.at[1, s, u])

        return carry

    lax.fori_loop(0, H, left_z, 0)

    def left_pairs(p, carry):
        left(tok.at[0], sb_s.at[p], sb_r.at[p])
        left(sib.at[0], cs_s.at[p], cs_r.at[p])
        return carry

    lax.fori_loop(0, Z, left_pairs, 0)
    for j in range(2):
        for i, w in enumerate((w_gate, w_up, w_down)):
            left(w.at[j], w_s.at[j, i], w_r.at[j, i])
        for k in range(1, SIDE):
            left(rows.at[j, pl.ds(0, H)], a_s.at[j, k], a_r.at[j, k])
            left(vsum.at[j, k], c_s.at[j, k], c_r.at[j, k])
        for k in range(SIDE):
            left(gath.at[j, 0], b_s.at[j, k, 0], b_r.at[j, k, 0])
            left(gath.at[j, 0], b_s.at[j, k, 1], b_r.at[j, k, 1])
            left(gath.at[j, 0], f_s.at[j, k], f_r.at[j, k])
            left(hop.at[j, 0], r1_s.at[j, k], r1_r.at[j, k])
        for k in range(2):
            left(hop.at[j, 0], r2_s.at[j, k], r2_r.at[j, k])


def body(hidden_in, norm_gain, expert_ids, route_weights, w_gate, w_up, w_down):
    n, wide = hidden_in.shape
    topk = expert_ids.shape[1]
    fh = w_gate.shape[1]
    groups = lax.axis_size("expert")
    Z = groups // 2
    H = Z // 2
    capacity = min(n, 3 * n * topk // (2 * 2 * groups))
    two = 2 * capacity
    route = jnp.concatenate([expert_ids.astype(F32), route_weights], axis=1).T
    vm, dma = pltpu.VMEM, pltpu.SemaphoreType.DMA
    shards = SIDE * SIDE
    scratch = [
        vm((groups, n + 2 * topk, wide), BF),
        vm((2, Z, two, wide), BF),
        vm((2, shards, H, two, wide), BF),
        vm((2, 3, 2 * fh, shards * wide), BF),
        vm((2, H * two, 2 * fh), F32),
        vm((2, H * two, 2 * fh), F32),
        vm((2, H * two, 2 * fh), BF),
        vm((2, shards, H, two, wide), BF),
        vm((2, 2, SIDE, H // 2, two, wide), BF),
        vm((2, SIDE, H, two, wide), BF),
        vm((2, SIDE, H, two, wide), BF),
        vm((2, SIDE, H, two, wide), BF),
        vm((2, SIDE, H, two, wide), BF),
        vm((2, Z, two, wide), BF),
        vm((Z, 4 * two, 2 * n), BF),
        vm((Z, 2, n, wide), BF),
        vm((Z, n, wide), BF),
        vm((2, H, n, wide), BF),
        vm((2, SIDE, 8, n), F32),
        dma((2, SIDE)), dma((2, SIDE)),
        dma((2, H)), dma((2, H)),
        dma((Z,)), dma((Z,)),
        dma((2, 3)), dma((2, 3)), dma((2, 3)),
        dma((2, SIDE)), dma((2, SIDE)),
        dma((2, SIDE, 2)), dma((2, SIDE, 2)),
        dma((2, SIDE)), dma((2, SIDE)),
        dma((2, SIDE)), dma((2, SIDE)),
        dma((2, 2)), dma((2, 2)),
        dma((2, SIDE)), dma((2, SIDE)),
        dma((Z,)), dma((Z,)),
        dma((2, H, 2)), dma((2, H, 2)),
    ]
    vmem = pl.BlockSpec(memory_space=pltpu.VMEM)
    anywhere = pl.BlockSpec(memory_space=pl.ANY)
    return pl.pallas_call(
        functools.partial(kernel, Z, capacity, wide * shards),
        out_shape=jax.ShapeDtypeStruct((n, wide), BF),
        in_specs=[vmem, vmem, vmem, anywhere, anywhere, anywhere],
        out_specs=vmem,
        scratch_shapes=scratch,
        compiler_params=pltpu.CompilerParams(
            collective_id=0, has_side_effects=True, vmem_limit_bytes=58 * 2**20
        ),
    )(hidden_in, norm_gain[None, :], route, w_gate, w_up, w_down)


def solution(mesh):
    placed = (
        P("expert", "tensor"),
        P("tensor"),
        P("expert", None),
        P("expert", None),
        P("expert", "tensor", None),
        P("expert", "tensor", None),
        P("expert", "tensor", None),
    )
    return jax.shard_map(
        body, mesh=mesh, in_specs=placed, out_specs=P("expert", "tensor"), check_vma=False
    )
```

time: 492 us -> 162 us (0.33)
  waiting for transfers between devices: 371 us -> 0 us
  Pallas kernels: 0 us -> 158 us
  blocking collectives: 69.7 us -> 0 us
  matrix products: 31.7 us -> 0 us
  between operations: 13.2 us -> 0.01 us
    reduce_scatter x2 -> x0, waiting for transfers between devices: 219 us -> none  [the longest x1 110 us: body(): lax.psum_scatter(weighted, 'expert', scatter_dimension=0, tiled=False)]
    pallas_call x0 -> x1, Pallas kernels: none -> 158 us  [body(): pl.pallas_call(functools.partial(kernel, Z, capacity, wide * shards), out...]
    all_gather x2 -> x0, waiting for transfers between devices: 152 us -> none  [the longest x1 112 us: body(): piece = lax.all_gather(rows, 'tensor', axis=2, tiled=True)]
    psum x1 -> x0, blocking collectives: 37.4 us -> none  [body(): squares = lax.psum(jnp.sum(widened * widened, axis=1), 'tensor')]
    all_gather x1 -> x0, blocking collectives: 32.3 us -> none  [body(): routing = lax.all_gather(routing.T, 'expert', axis=0, tiled=False)]
    dot_general x5 -> x0, matrix products: 31.7 us -> none  [the longest x1 15.3 us: body(): jnp.einsum('erf,efd->erd', inner, w_down, preferred_element_type=jnp.floa...]
  transfers between devices with their start and end apart: 4 -> 0, of which waited for: 4 -> 0; matrix products, arithmetic and copies ran while one was open for 0% -> 0% of each run, Pallas kernels for 0% -> 0%
where the time goes in v2:
time: 162 us; the launch traced here: 161 us
  Pallas kernels  158 us (98%)
  other arithmetic  1.97 us (1%)
    pallas_call x1, Pallas kernels, body(): pl.pallas_call(functools.partial(kernel, Z, capacity, wide * shards), out...  158 us

profile of v2, /device:TPU:6, one launch (start us, length us, event | category | flops | bytes accessed | tf_op | source)
XLA Modules:
  0.0 161.4 jit_solution(1630878776720821154)
XLA Ops:
  0.0 0.7 convert_element_type.3
  0.7 1.3 maximum_bitcast_fusion.route
  2.0 158.0 %shard_map.73 = bf16[128,256]{1,0:T(8,128)(2,1)} custom-call(bf16[128,256]{1,0:T(8,128)(2,1)} %hid.1, f32[1,256]{1,0:T(1,128)} %bitcast.3, f32[16,128]{1,0:T(8,128)} %maximum_bitcast_fusion.route, bf16[2,96,4096]{2,1,0:T(8,128)(2,1)} %w_gate.1, bf16[2,96,4096]{2,1,0:T(8,128)(2,1)} %w_up.1, bf16[2,96,4096]{2,1,0:T(8,128)(2,1)} %w_down.1), custom_call_target="tpu_custom_call" | custom-call | tf_op jit(solution)/shard_map/pallas_call | solution.py:529
  160.0 1.5 copy.9

commit v3 on v1

v3 whole, which is shorter than its diff:
```python
import functools

import jax
import jax.numpy as jnp
from jax import lax
from jax.experimental import pallas as pl
from jax.experimental.pallas import tpu as pltpu
from jax.sharding import PartitionSpec as P

epsilon = 1e-06
SIDE = 4
BF = jnp.bfloat16
F32 = jnp.float32


def dot(a, b, ca, cb):
    return lax.dot_general(a, b, (((ca,), (cb,)), ((), ())), preferred_element_type=F32)


def kernel(
    Z, capacity, width,
    hid, gain, ids_in, weights_in, w_gate, w_up, w_down, out,
    tok, rows, gath, wts, accg, accu, ssq, inner, part, hop, from_l, from_r, vsum, cross, final,
    sw, cont, sib, zin, gains,
    gn_s, gn_r, za_s, za_r, sb_s, sb_r, wl_r, w_s, w_r, a_s, a_r, b_s, b_r, f_s, f_r,
    r1_s, r1_r, r2_s, r2_r, c_s, c_r, cs_s, cs_r, q_s, q_r,
):
    H = Z // 2
    Q = H // 2
    A = Q // 2
    n, wide = hid.shape
    fh = w_gate.shape[1]
    topk = ids_in.shape[1]
    experts = 4 * Z
    two = 2 * capacity
    chunk_rows = Q * two
    mesh_ids = pl.DeviceIdType.MESH

    E = lax.axis_index("expert")
    T = lax.axis_index("tensor")
    z, c = lax.div(E, 2), lax.rem(E, 2)
    y, x = lax.div(T, SIDE), lax.rem(T, SIDE)

    def mod(v, m):
        return lax.rem(v + m, m)

    def axes(j):
        return (x + j * (y - x), y + j * (x - y))

    def device(j, a, b):
        return (E, (b + j * (a - b)) * SIDE + a + j * (b - a))

    def owner(j, sh):
        bb, aa = lax.div(sh, SIDE), lax.rem(sh, SIDE)
        return bb * SIDE + aa + j * (aa * SIDE + bb - bb * SIDE - aa)

    def column(j, sh):
        return pl.ds(pl.multiple_of(owner(j, sh) * wide, wide), wide)

    def send(src, dst, ssem, rsem, to):
        pltpu.make_async_remote_copy(
            src_ref=src, dst_ref=dst, send_sem=ssem, recv_sem=rsem,
            device_id=to, device_id_type=mesh_ids,
        ).start()

    def got(dst, ssem, rsem):
        pltpu.make_async_remote_copy(
            src_ref=dst, dst_ref=dst, send_sem=ssem, recv_sem=rsem,
            device_id=(E, T), device_id_type=mesh_ids,
        ).wait_recv()

    def left(src, ssem, rsem):
        pltpu.make_async_remote_copy(
            src_ref=src, dst_ref=src, send_sem=ssem, recv_sem=rsem,
            device_id=(E, T), device_id_type=mesh_ids,
        ).wait_send()

    other = (2 * z + 1 - c, T)
    z_up = (2 * mod(z + 1, Z) + c, T)
    z_down = (2 * mod(z - 1, Z) + c, T)

    barrier = pltpu.get_barrier_semaphore()
    partners = [other, z_up, z_down]
    for m in range(1, SIDE):
        partners.append((E, y * SIDE + mod(x + m, SIDE)))
        partners.append((E, mod(y + m, SIDE) * SIDE + x))
    for partner in partners:
        pl.semaphore_signal(barrier, inc=1, device_id=partner, device_id_type=mesh_ids)

    ids = ids_in[...].astype(F32).T
    wts_t = weights_in[...].T
    e_iota = lax.broadcasted_iota(jnp.int32, (experts, n), 0).astype(F32)
    hits = [e_iota == ids[k : k + 1, :] for k in range(topk)]
    chosen = jnp.zeros((experts, n), F32)
    for k in range(topk):
        chosen = chosen + jnp.where(hits[k], 1.0, 0.0)
    tri = (
        lax.broadcasted_iota(jnp.int32, (n, n), 0) < lax.broadcasted_iota(jnp.int32, (n, n), 1)
    ).astype(F32).astype(BF)
    before = dot(chosen.astype(BF), tri, 1, 0)
    pos = jnp.concatenate(
        [jnp.sum(jnp.where(hits[k], before, 0.0), axis=0, keepdims=True) for k in range(topk)],
        axis=0,
    )
    high = wts_t.astype(BF).astype(F32)
    meta = jnp.concatenate(
        [jnp.concatenate([ids, high], axis=1), jnp.concatenate([wts_t - high, pos], axis=1)],
        axis=0,
    )
    tok[E, n : n + 2 * topk, :] = meta.astype(BF)
    tok[E, 0:n, :] = hid[...]
    gains[T] = jnp.broadcast_to(gain[...], (8, wide))
    for j in range(2):
        for i, w in enumerate((w_gate, w_up, w_down)):
            pltpu.make_async_copy(w.at[j], wts.at[j, i, pl.ds(0, fh)], wl_r.at[j, i]).start()
    pl.semaphore_wait(barrier, len(partners))

    nb = 16 * ((n + 2 * topk + 31) // 32)
    cuts = [pl.ds(0, nb), pl.ds(nb, n + 2 * topk - nb)]
    for u in range(2):
        mine = tok.at[E, cuts[u]]
        send(mine, mine, za_s.at[0, 0, u], za_r.at[0, 0, u], z_up)
        send(mine, mine, za_s.at[1, 0, u], za_r.at[1, 0, u], z_down)
    send(tok.at[E], tok.at[E], sb_s.at[0], sb_r.at[0], other)
    for m in range(1, SIDE):
        to = (E, y * SIDE + mod(x + m, SIDE))
        send(gains.at[T], gains.at[T], gn_s.at[0, m], gn_r.at[0, m], to)

    for j in range(2):
        a, b = axes(j)
        mate = mod(a + 1 - 2 * lax.rem(a + c, 2), SIDE)
        for i, w in enumerate((w_gate, w_up, w_down)):
            send(w.at[j], wts.at[j, i, pl.ds(fh, fh)], w_s.at[j, i], w_r.at[j, i], device(j, mate, b))

    for m in range(1, SIDE):
        got(gains.at[y * SIDE + mod(x - m, SIDE)], gn_s.at[0, m], gn_r.at[0, m])
    line = gains.at[pl.ds(y * SIDE, SIDE)]
    for m in range(1, SIDE):
        to = (E, mod(y + m, SIDE) * SIDE + x)
        send(line, line, gn_s.at[1, m], gn_r.at[1, m], to)

    r_iota = lax.broadcasted_iota(jnp.int32, (two, 2 * n), 0).astype(F32)
    lane = lax.broadcasted_iota(jnp.int32, (1, 2 * n), 1)
    shift = jnp.where(lane >= n, float(capacity), 0.0)
    here = (2 * E).astype(F32)

    def select(r):
        p = mod(jnp.where(r < H, z + r, z + H - 1 - r), Z)
        got(tok.at[2 * p + 1 - c], sb_s.at[r], sb_r.at[r])
        m0 = tok[2 * p, n : n + 2 * topk, :].astype(F32)
        m1 = tok[2 * p + 1, n : n + 2 * topk, :].astype(F32)

        def both(i, l):
            return jnp.concatenate(
                [
                    m0[i * topk : (i + 1) * topk, l * n : (l + 1) * n],
                    m1[i * topk : (i + 1) * topk, l * n : (l + 1) * n],
                ],
                axis=1,
            )

        idp, high, low, pos = both(0, 0), both(0, 1), both(1, 0), both(1, 1)
        picked = []
        for j in range(2):
            hit = idp == here + float(j)
            named = jnp.sum(jnp.where(hit, 1.0, 0.0), axis=0, keepdims=True)
            slot = jnp.sum(jnp.where(hit, pos, 0.0), axis=0, keepdims=True)
            wh = jnp.sum(jnp.where(hit, high, 0.0), axis=0, keepdims=True)
            wo = jnp.sum(jnp.where(hit, low, 0.0), axis=0, keepdims=True)
            slot = jnp.where(named > 0.5, slot + shift, -1.0)
            taken = jnp.where(r_iota == slot, 1.0, 0.0)
            sw[r, j * two : (j + 1) * two, :] = (taken * wh).astype(BF)
            sw[r, (2 + j) * two : (3 + j) * two, :] = (taken * wo).astype(BF)
            picked.append(taken.astype(BF))
        pair = tok[pl.ds(2 * p, 2), 0:n, :].reshape(2 * n, wide)
        taken = dot(jnp.concatenate(picked, axis=0), pair, 1, 0).astype(BF)
        rows[0, r] = taken[0:two, :]
        rows[1, r] = taken[two : 2 * two, :]

    def z_step(s, carry):
        pr, po = mod(z - 1 - s, Z), mod(z + 1 + s, Z)
        er, eo = 2 * pr + c, 2 * po + c
        for u in range(2):
            br, bo = tok.at[er, cuts[u]], tok.at[eo, cuts[u]]
            got(br, za_s.at[0, s, u], za_r.at[0, s, u])

            @pl.when(s < H - 1)
            def _():
                send(br, br, za_s.at[0, s + 1, u], za_r.at[0, s + 1, u], z_up)
                got(bo, za_s.at[1, s, u], za_r.at[1, s, u])

            @pl.when(s < H - 2)
            def _():
                send(bo, bo, za_s.at[1, s + 1, u], za_r.at[1, s + 1, u], z_down)

        send(tok.at[er], tok.at[er], sb_s.at[H + s], sb_r.at[H + s], other)

        @pl.when(s < H - 1)
        def _():
            send(tok.at[eo], tok.at[eo], sb_s.at[s + 1], sb_r.at[s + 1], other)

        select(s)

        @pl.when(s > 0)
        def _():
            select(H + s - 1)

        return carry

    lax.fori_loop(0, H, z_step, 0)
    select(Z - 1)

    def mine_of(j, ch, half):
        return rows.at[j, pl.ds(H * half + Q * ch, Q)]

    for ch in (1, 0):
        for j in range(2):
            a, b = axes(j)
            sh = b * SIDE + a
            pltpu.make_async_copy(
                mine_of(j, ch, lax.rem(a, 2)), gath.at[j, ch, sh], a_r.at[j, ch, 0]
            ).start()
            for k in (1, 3, 2):
                to = mod(a - k, SIDE)
                send(
                    mine_of(j, ch, lax.rem(to, 2)), gath.at[j, ch, sh],
                    a_s.at[j, ch, k], a_r.at[j, ch, k], device(j, to, b),
                )

    def forward(j, ch, k):
        a, b = axes(j)
        piece = gath.at[j, ch, b * SIDE + mod(a + k, SIDE)]
        for way, d in ((0, 1), (1, -1)):
            send(
                piece, piece, b_s.at[j, ch, k, way], b_r.at[j, ch, k, way],
                device(j, a, mod(b + d, SIDE)),
            )

    def near(ch):
        for j in range(2):
            a, b = axes(j)
            pltpu.make_async_copy(
                mine_of(j, ch, lax.rem(a, 2)), gath.at[j, ch, b * SIDE + a], a_r.at[j, ch, 0]
            ).wait()
            forward(j, ch, 0)

        def step(i, carry):
            j, k = lax.rem(i, 2), lax.div(i, 2)
            a, b = axes(j)
            sh = b * SIDE + mod(a + k, SIDE)
            got(gath.at[j, ch, sh], a_s.at[j, ch, k], a_r.at[j, ch, k])
            forward(j, ch, k)
            return carry

        lax.fori_loop(2, 2 * SIDE, step, 0)

    def multiply(j, ch, sh):
        piece = gath[j, ch, sh].reshape(chunk_rows, wide).astype(F32)
        ssq[j, ch] += piece * piece
        piece = (piece * gains[owner(j, sh), 0:1, :]).astype(BF)
        col = column(j, sh)
        accg[j, ch] += dot(piece, wts[j, 0, :, col], 1, 1)
        accu[j, ch] += dot(piece, wts[j, 1, :, col], 1, 1)

    def multiply_near(ch):
        def step(i, carry):
            j, k = lax.rem(i, 2), lax.div(i, 2)
            multiply(j, ch, axes(j)[1] * SIDE + k)
            return carry

        lax.fori_loop(0, 2 * SIDE, step, 0)

    def side(ch, work):
        def step(i, carry):
            j, k = lax.rem(i, 2), lax.div(i, 2)
            a, b = axes(j)
            low = mod(b - 1, SIDE) * SIDE + mod(a + k, SIDE)
            high = mod(b + 1, SIDE) * SIDE + mod(a + k, SIDE)
            got(gath.at[j, ch, low], b_s.at[j, ch, k, 0], b_r.at[j, ch, k, 0])

            @pl.when(lax.rem(k, 2) == 0)
            def _():
                piece = gath.at[j, ch, low]
                to = device(j, a, mod(b + 1, SIDE))
                send(piece, piece, f_s.at[j, ch, k], f_r.at[j, ch, k], to)

            got(gath.at[j, ch, high], b_s.at[j, ch, k, 1], b_r.at[j, ch, k, 1])

            @pl.when(lax.rem(k, 2) == 1)
            def _():
                piece = gath.at[j, ch, high]
                to = device(j, a, mod(b - 1, SIDE))
                send(piece, piece, f_s.at[j, ch, k], f_r.at[j, ch, k], to)

            if work:
                multiply(j, ch, low)
                multiply(j, ch, high)
            return carry

        lax.fori_loop(0, 2 * SIDE, step, 0)

    def multiply_side(ch):
        def step(i, carry):
            j, k = lax.rem(i, 2), lax.div(i, 2)
            b = axes(j)[1]
            multiply(j, ch, mod(b - 1, SIDE) * SIDE + k)
            multiply(j, ch, mod(b + 1, SIDE) * SIDE + k)
            return carry

        lax.fori_loop(0, 2 * SIDE, step, 0)

    def far(ch):
        def step(i, carry):
            j, k = lax.rem(i, 2), lax.div(i, 2)
            a, b = axes(j)
            sh = mod(b + 2, SIDE) * SIDE + mod(a + k, SIDE)
            got(gath.at[j, ch, sh], f_s.at[j, ch, k], f_r.at[j, ch, k])
            multiply(j, ch, sh)
            return carry

        lax.fori_loop(0, 2 * SIDE, step, 0)

    def activate(ch):
        for j in range(2):
            total = jnp.sum(ssq[j, ch], axis=1, keepdims=True)
            scale = lax.rsqrt(total / width + epsilon)
            g = accg[j, ch] * scale
            inner[j, ch] = (g / (1.0 + jnp.exp(-g)) * (accu[j, ch] * scale)).astype(BF)

    lo, hi = pl.ds(0, A), pl.ds(A, A)

    def ends(j):
        a, b = axes(j)
        return device(j, a, mod(b + 1, SIDE)), device(j, a, mod(b - 1, SIDE))

    def down(ch):
        for d in (2, 1, 3, 0):

            def step(i, carry, d=d):
                j, aa = lax.rem(i, 2), lax.div(i, 2)
                sh = mod(axes(j)[1] + d, SIDE) * SIDE + aa
                made = dot(inner[j, ch], wts[j, 2, :, column(j, sh)], 1, 0).astype(BF)
                part[j, ch, sh] = made.reshape(Q, two, wide)
                return carry

            lax.fori_loop(0, 2 * SIDE, step, 0)
            for j in range(2):
                above, below = ends(j)
                bundle = part.at[j, ch, pl.ds(mod(axes(j)[1] + d, SIDE) * SIDE, SIDE)]
                ss, rs = r1_s.at[j, ch], r1_r.at[j, ch]
                if d == 2:
                    send(bundle.at[:, lo], hop.at[j, ch, 0], ss.at[0], rs.at[0], above)
                    send(bundle.at[:, hi], hop.at[j, ch, 1], ss.at[1], rs.at[1], below)
                elif d == 1:
                    send(bundle.at[:, hi], from_l.at[j, ch, :, hi], ss.at[2], rs.at[2], above)
                elif d == 3:
                    send(bundle.at[:, lo], from_r.at[j, ch, :, lo], ss.at[3], rs.at[3], below)

    def hops(ch):
        for way, (d, cut, target) in enumerate(((1, lo, from_l), (3, hi, from_r))):
            for j in range(2):
                first = mod(axes(j)[1] + d, SIDE) * SIDE
                got(hop.at[j, ch, way], r1_s.at[j, ch, way], r1_r.at[j, ch, way])

                def step(aa, carry, j=j, first=first, cut=cut, way=way):
                    mixed = part[j, ch, first + aa, cut].astype(F32) + hop[j, ch, way, aa].astype(
                        F32
                    )
                    part[j, ch, first + aa, cut] = mixed.astype(BF)
                    return carry

                lax.fori_loop(0, SIDE, step, 0)
                send(
                    part.at[j, ch, pl.ds(first, SIDE), cut], target.at[j, ch, :, cut],
                    r2_s.at[j, ch, way], r2_r.at[j, ch, way], ends(j)[way],
                )

    def columns(ch):
        for j in range(2):
            a, b = axes(j)
            got(from_l.at[j, ch, :, hi], r1_s.at[j, ch, 2], r1_r.at[j, ch, 2])
            got(from_r.at[j, ch, :, lo], r1_s.at[j, ch, 3], r1_r.at[j, ch, 3])
            got(from_l.at[j, ch, :, lo], r2_s.at[j, ch, 0], r2_r.at[j, ch, 0])
            got(from_r.at[j, ch, :, hi], r2_s.at[j, ch, 1], r2_r.at[j, ch, 1])

            def step(i, carry, j=j, a=a, b=b):
                m = lax.rem(SIDE + 2 - i, SIDE)
                aa = mod(a + m, SIDE)
                mixed = (
                    part[j, ch, b * SIDE + aa].astype(F32)
                    + from_l[j, ch, aa].astype(F32)
                    + from_r[j, ch, aa].astype(F32)
                )
                vsum[j, ch, m] = mixed.astype(BF)

                @pl.when(m > 0)
                def _():
                    send(
                        vsum.at[j, ch, m], cross.at[j, ch, m], c_s.at[j, ch, m],
                        c_r.at[j, ch, m], device(j, aa, b),
                    )

                return carry

            lax.fori_loop(0, SIDE, step, 0)

    def finish(ch):
        for j in range(2):
            own = lax.rem(axes(j)[0], 2)
            for m in (1, 3, 2):
                got(cross.at[j, ch, m], c_s.at[j, ch, m], c_r.at[j, ch, m])
            final[j, pl.ds(H * (1 - own) + Q * ch, Q)] = (
                cross[j, ch, 1].astype(F32) + cross[j, ch, 3].astype(F32)
            ).astype(BF)
            final[j, pl.ds(H * own + Q * ch, Q)] = (
                vsum[j, ch, 0].astype(F32) + cross[j, ch, 2].astype(F32)
            ).astype(BF)

    accg[...] = jnp.zeros_like(accg)
    accu[...] = jnp.zeros_like(accu)
    ssq[...] = jnp.zeros_like(ssq)
    near(1)
    for m in range(1, SIDE):
        got(gains.at[pl.ds(mod(y - m, SIDE) * SIDE, SIDE)], gn_s.at[1, m], gn_r.at[1, m])
    for j in range(2):
        for i, w in enumerate((w_gate, w_up, w_down)):
            pltpu.make_async_copy(w.at[j], wts.at[j, i, pl.ds(0, fh)], wl_r.at[j, i]).wait()
            got(wts.at[j, i, pl.ds(fh, fh)], w_s.at[j, i], w_r.at[j, i])
    near(0)
    multiply_near(1)
    side(1, True)
    side(0, False)
    multiply_near(0)
    far(1)
    activate(1)
    down(1)
    multiply_side(0)
    far(0)
    activate(0)
    hops(1)
    down(0)

    def combine(r):
        stacked = jnp.concatenate([final[0, r], final[1, r]], axis=0)
        stacked = jnp.concatenate([stacked, stacked], axis=0)
        made = dot(sw[r], stacked, 0, 0).astype(BF)
        cont[r, 0] = made[0:n, :]
        cont[r, 1] = made[n : 2 * n, :]
        send(cont.at[r, 1 - c], sib.at[r], cs_s.at[r], cs_r.at[r], other)

    hn = n // 2

    def pass_on(way, s, r, to):
        got(sib.at[r], cs_s.at[r], cs_r.at[r])
        for u in range(2):
            cut = pl.ds(u * hn, hn)

            @pl.when(s == 0)
            def _():
                cont[r, c, cut] = (cont[r, c, cut].astype(F32) + sib[r, cut].astype(F32)).astype(BF)

            @pl.when(s > 0)
            def _():
                got(zin.at[way, s - 1, cut], q_s.at[way, s - 1, u], q_r.at[way, s - 1, u])
                cont[r, c, cut] = (
                    cont[r, c, cut].astype(F32)
                    + sib[r, cut].astype(F32)
                    + zin[way, s - 1, cut].astype(F32)
                ).astype(BF)

            send(
                cont.at[r, c, cut], zin.at[way, s, cut], q_s.at[way, s, u], q_r.at[way, s, u], to
            )

    def place_right(s):
        return jnp.where(s == 0, Z - 1, H - s)

    def ring_first(s, carry):
        @pl.when(s < Q)
        def _():
            combine(H - 1 - s)

            @pl.when(s < Q - 1)
            def _():
                combine(Z - 2 - s)

        pass_on(0, s, place_right(s), z_up)

        @pl.when((s > 0) & (s < Q))
        def _():
            pass_on(1, s - 1, Z - 1 - s, z_down)

        return carry

    def ring_last(s, carry):
        pass_on(1, s - 2, Z - s, z_down)

        @pl.when(s < H)
        def _():
            combine(H - 1 - s)
            pass_on(0, s, H - s, z_up)

        @pl.when(s < H)
        def _():
            combine(Z - 1 - s)

        return carry

    columns(1)
    finish(1)
    combine(Z - 1)
    lax.fori_loop(0, 2, ring_first, 0)
    hops(0)
    lax.fori_loop(2, Q, ring_first, 0)
    columns(0)
    lax.fori_loop(Q, Q + 1, ring_first, 0)
    finish(0)
    combine(H + Q - 1)
    combine(Q - 1)
    lax.fori_loop(Q + 1, H + 1, ring_last, 0)
    got(sib.at[0], cs_s.at[0], cs_r.at[0])
    for u in range(2):
        cut = pl.ds(u * hn, hn)
        got(zin.at[1, H - 2, cut], q_s.at[1, H - 2, u], q_r.at[1, H - 2, u])
        got(zin.at[0, H - 1, cut], q_s.at[0, H - 1, u], q_r.at[0, H - 1, u])
        out[cut] = (
            cont[0, c, cut].astype(F32)
            + sib[0, cut].astype(F32)
            + zin[1, H - 2, cut].astype(F32)
            + zin[0, H - 1, cut].astype(F32)
        ).astype(BF)

    for m in range(1, SIDE):
        left(gains.at[0], gn_s.at[0, m], gn_r.at[0, m])
        left(line, gn_s.at[1, m], gn_r.at[1, m])

    def left_z(s, carry):
        for u in range(2):
            left(tok.at[0, cuts[u]], za_s.at[0, s, u], za_r.at[0, s, u])
            cut = pl.ds(u * hn, hn)
            left(zin.at[0, 0, cut], q_s.at[0, s, u], q_r.at[0, s, u])

            @pl.when(s < H - 1)
            def _():
                left(tok.at[0, cuts[u]], za_s.at[1, s, u], za_r.at[1, s, u])
                left(zin.at[1, 0, cut], q_s.at[1, s, u], q_r.at[1, s, u])

        return carry

    lax.fori_loop(0, H, left_z, 0)

    def left_pairs(r, carry):
        left(tok.at[0], sb_s.at[r], sb_r.at[r])
        left(sib.at[0], cs_s.at[r], cs_r.at[r])
        return carry

    lax.fori_loop(0, Z, left_pairs, 0)
    for j in range(2):
        for i, w in enumerate((w_gate, w_up, w_down)):
            left(w.at[j], w_s.at[j, i], w_r.at[j, i])

    def left_pieces(i, carry):
        j, ch, k = lax.rem(i, 2), lax.rem(lax.div(i, 2), 2), lax.div(i, 4)
        piece = gath.at[j, ch, 0]

        @pl.when(k > 0)
        def _():
            left(piece, a_s.at[j, ch, k], a_r.at[j, ch, k])
            left(piece, c_s.at[j, ch, k], c_r.at[j, ch, k])

        left(piece, b_s.at[j, ch, k, 0], b_r.at[j, ch, k, 0])
        left(piece, b_s.at[j, ch, k, 1], b_r.at[j, ch, k, 1])
        left(piece, f_s.at[j, ch, k], f_r.at[j, ch, k])
        left(hop.at[j, ch, 0], r1_s.at[j, ch, k], r1_r.at[j, ch, k])

        @pl.when(k < 2)
        def _():
            left(hop.at[j, ch, 0], r2_s.at[j, ch, k], r2_r.at[j, ch, k])

        return carry

    lax.fori_loop(0, 4 * SIDE, left_pieces, 0)


def body(hidden_in, norm_gain, expert_ids, route_weights, w_gate, w_up, w_down):
    n, wide = hidden_in.shape
    topk = expert_ids.shape[1]
    fh = w_gate.shape[1]
    groups = lax.axis_size("expert")
    Z = groups // 2
    H, Q = Z // 2, Z // 4
    capacity = min(n, 3 * n * topk // (2 * 2 * groups))
    two = 2 * capacity
    vm, dma = pltpu.VMEM, pltpu.SemaphoreType.DMA
    shards = SIDE * SIDE
    scratch = [
        vm((groups, n + 2 * topk, wide), BF),
        vm((2, Z, two, wide), BF),
        vm((2, 2, shards, Q, two, wide), BF),
        vm((2, 3, 2 * fh, shards * wide), BF),
        vm((2, 2, Q * two, 2 * fh), F32),
        vm((2, 2, Q * two, 2 * fh), F32),
        vm((2, 2, Q * two, wide), F32),
        vm((2, 2, Q * two, 2 * fh), BF),
        vm((2, 2, shards, Q, two, wide), BF),
        vm((2, 2, 2, SIDE, Q // 2, two, wide), BF),
        vm((2, 2, SIDE, Q, two, wide), BF),
        vm((2, 2, SIDE, Q, two, wide), BF),
        vm((2, 2, SIDE, Q, two, wide), BF),
        vm((2, 2, SIDE, Q, two, wide), BF),
        vm((2, Z, two, wide), BF),
        vm((Z, 4 * two, 2 * n), BF),
        vm((Z, 2, n, wide), BF),
        vm((Z, n, wide), BF),
        vm((2, H, n, wide), BF),
        vm((shards, 8, wide), F32),
        dma((2, SIDE)), dma((2, SIDE)),
        dma((2, H, 2)), dma((2, H, 2)),
        dma((Z,)), dma((Z,)),
        dma((2, 3)), dma((2, 3)), dma((2, 3)),
        dma((2, 2, SIDE)), dma((2, 2, SIDE)),
        dma((2, 2, SIDE, 2)), dma((2, 2, SIDE, 2)),
        dma((2, 2, SIDE)), dma((2, 2, SIDE)),
        dma((2, 2, SIDE)), dma((2, 2, SIDE)),
        dma((2, 2, 2)), dma((2, 2, 2)),
        dma((2, 2, SIDE)), dma((2, 2, SIDE)),
        dma((Z,)), dma((Z,)),
        dma((2, H, 2)), dma((2, H, 2)),
    ]
    vmem = pl.BlockSpec(memory_space=pltpu.VMEM)
    anywhere = pl.BlockSpec(memory_space=pl.ANY)
    return pl.pallas_call(
        functools.partial(kernel, Z, capacity, wide * shards),
        out_shape=jax.ShapeDtypeStruct((n, wide), BF),
        in_specs=[vmem, vmem, vmem, vmem, anywhere, anywhere, anywhere],
        out_specs=vmem,
        scratch_shapes=scratch,
        compiler_params=pltpu.CompilerParams(
            collective_id=0, has_side_effects=True, vmem_limit_bytes=58 * 2**20
        ),
    )(hidden_in, norm_gain[None, :], expert_ids, route_weights, w_gate, w_up, w_down)


def solution(mesh):
    placed = (
        P("expert", "tensor"),
        P("tensor"),
        P("expert", None),
        P("expert", None),
        P("expert", "tensor", None),
        P("expert", "tensor", None),
        P("expert", "tensor", None),
    )
    return jax.shard_map(
        body, mesh=mesh, in_specs=placed, out_specs=P("expert", "tensor"), check_vma=False
    )
```

time: 492 us -> 148 us (0.30)
  waiting for transfers between devices: 371 us -> 0 us
  Pallas kernels: 0 us -> 142 us
  blocking collectives: 69.7 us -> 0 us
  matrix products: 31.7 us -> 0 us
  between operations: 13.2 us -> 0.01 us
    reduce_scatter x2 -> x0, waiting for transfers between devices: 219 us -> none  [the longest x1 110 us: body(): lax.psum_scatter(weighted, 'expert', scatter_dimension=0, tiled=False)]
    all_gather x2 -> x0, waiting for transfers between devices: 152 us -> none  [the longest x1 112 us: body(): piece = lax.all_gather(rows, 'tensor', axis=2, tiled=True)]
    pallas_call x0 -> x1, Pallas kernels: none -> 142 us  [body(): pl.pallas_call(functools.partial(kernel, Z, capacity, wide * shards), out...]
    psum x1 -> x0, blocking collectives: 37.4 us -> none  [body(): squares = lax.psum(jnp.sum(widened * widened, axis=1), 'tensor')]
    all_gather x1 -> x0, blocking collectives: 32.3 us -> none  [body(): routing = lax.all_gather(routing.T, 'expert', axis=0, tiled=False)]
    dot_general x5 -> x0, matrix products: 31.7 us -> none  [the longest x1 15.3 us: body(): jnp.einsum('erf,efd->erd', inner, w_down, preferred_element_type=jnp.floa...]
  transfers between devices with their start and end apart: 4 -> 0, of which waited for: 4 -> 0; matrix products, arithmetic and copies ran while one was open for 0% -> 0% of each run, Pallas kernels for 0% -> 0%
where the time goes in v3:
time: 148 us; the launch traced here: 147 us
  Pallas kernels  142 us (96%)
  local copies, waits for them, and re-layouts  4.29 us (3%)
    pallas_call x1, Pallas kernels, body(): pl.pallas_call(functools.partial(kernel, Z, capacity, wide * shards), out...  142 us
    unnamed x3, local copies, waits for them, and re-layouts  4.29 us

profile of v3, /device:TPU:6, one launch (start us, length us, event | category | flops | bytes accessed | tf_op | source)
XLA Modules:
  0.0 146.5 jit_solution(9565520622878003846)
XLA Ops:
  0.0 1.4 copy.8.ids_in
  1.4 1.4 copy.9.weights_in
  2.8 142.2 %shard_map.73 = bf16[128,256]{1,0:T(8,128)(2,1)} custom-call(bf16[128,256]{1,0:T(8,128)(2,1)} %hid.1, f32[1,256]{1,0:T(1,128)} %bitcast.1, s32[128,8]{1,0:T(8,128)} %copy.8.ids_in, f32[128,8]{1,0:T(8,128)} %copy.9.weights_in, bf16[2,96,4096]{2,1,0:T(8,128)(2,1)} %w_gate.1, bf16[2,96,4096]{2,1,0:T(8,128)(2,1)} %w_up.1, bf16[2,96,4096]{2,1,0:T(8,128)(2,1)} %w_down.1), custom_call_target="tpu_custom_call" | custom-call | tf_op jit(solution)/shard_map/pallas_call | solution.py:632
  145.0 1.5 %copy.11 = bf16[128,256]{1,0:T(8,128)(2,1)} copy(bf16[128,256]{1,0:T(8,128)(2,1)} %shard_map.73) | data formatting | bytes 131072

commit v4 on v3

--- a/solution.py
+++ b/solution.py
@@ -27,7 +27,7 @@
 ):
     H = Z // 2
     Q = H // 2
-    A = Q // 2
+    A = Q // 4
     n, wide = hid.shape
     fh = w_gate.shape[1]
     topk = ids_in.shape[1]
@@ -126,18 +126,11 @@
         to = (E, y * SIDE + mod(x + m, SIDE))
         send(gains.at[T], gains.at[T], gn_s.at[0, m], gn_r.at[0, m], to)
 
-    for j in range(2):
-        a, b = axes(j)
-        mate = mod(a + 1 - 2 * lax.rem(a + c, 2), SIDE)
-        for i, w in enumerate((w_gate, w_up, w_down)):
+    for i, w in enumerate((w_gate, w_up, w_down)):
+        for j in range(2):
+            a, b = axes(j)
+            mate = mod(a + 1 - 2 * lax.rem(a + c, 2), SIDE)
             send(w.at[j], wts.at[j, i, pl.ds(fh, fh)], w_s.at[j, i], w_r.at[j, i], device(j, mate, b))
-
-    for m in range(1, SIDE):
-        got(gains.at[y * SIDE + mod(x - m, SIDE)], gn_s.at[0, m], gn_r.at[0, m])
-    line = gains.at[pl.ds(y * SIDE, SIDE)]
-    for m in range(1, SIDE):
-        to = (E, mod(y + m, SIDE) * SIDE + x)
-        send(line, line, gn_s.at[1, m], gn_r.at[1, m], to)
 
     r_iota = lax.broadcasted_iota(jnp.int32, (two, 2 * n), 0).astype(F32)
     lane = lax.broadcasted_iota(jnp.int32, (1, 2 * n), 1)
@@ -207,13 +200,10 @@
 
         return carry
 
-    lax.fori_loop(0, H, z_step, 0)
-    select(Z - 1)
-
     def mine_of(j, ch, half):
         return rows.at[j, pl.ds(H * half + Q * ch, Q)]
 
-    for ch in (1, 0):
+    def scatter(ch):
         for j in range(2):
             a, b = axes(j)
             sh = b * SIDE + a
@@ -227,6 +217,18 @@
                     a_s.at[j, ch, k], a_r.at[j, ch, k], device(j, to, b),
                 )
 
+    lax.fori_loop(0, Q + 1, z_step, 0)
+    scatter(0)
+    for m in range(1, SIDE):
+        got(gains.at[y * SIDE + mod(x - m, SIDE)], gn_s.at[0, m], gn_r.at[0, m])
+    line = gains.at[pl.ds(y * SIDE, SIDE)]
+    for m in range(1, SIDE):
+        to = (E, mod(y + m, SIDE) * SIDE + x)
+        send(line, line, gn_s.at[1, m], gn_r.at[1, m], to)
+    lax.fori_loop(Q + 1, H, z_step, 0)
+    select(Z - 1)
+    scatter(1)
+
     def forward(j, ch, k):
         a, b = axes(j)
         piece = gath.at[j, ch, b * SIDE + mod(a + k, SIDE)]
@@ -327,118 +329,102 @@
             g = accg[j, ch] * scale
             inner[j, ch] = (g / (1.0 + jnp.exp(-g)) * (accu[j, ch] * scale)).astype(BF)
 
-    lo, hi = pl.ds(0, A), pl.ds(A, A)
+    def cuts_of(rc):
+        first = 2 * A * (rc % 2)
+        return pl.ds(first, A), pl.ds(first + A, A), pl.ds(first, 2 * A)
 
     def ends(j):
         a, b = axes(j)
         return device(j, a, mod(b + 1, SIDE)), device(j, a, mod(b - 1, SIDE))
 
-    def down(ch):
-        for d in (2, 1, 3, 0):
-
-            def step(i, carry, d=d):
-                j, aa = lax.rem(i, 2), lax.div(i, 2)
-                sh = mod(axes(j)[1] + d, SIDE) * SIDE + aa
-                made = dot(inner[j, ch], wts[j, 2, :, column(j, sh)], 1, 0).astype(BF)
-                part[j, ch, sh] = made.reshape(Q, two, wide)
-                return carry
-
-            lax.fori_loop(0, 2 * SIDE, step, 0)
-            for j in range(2):
-                above, below = ends(j)
-                bundle = part.at[j, ch, pl.ds(mod(axes(j)[1] + d, SIDE) * SIDE, SIDE)]
-                ss, rs = r1_s.at[j, ch], r1_r.at[j, ch]
-                if d == 2:
-                    send(bundle.at[:, lo], hop.at[j, ch, 0], ss.at[0], rs.at[0], above)
-                    send(bundle.at[:, hi], hop.at[j, ch, 1], ss.at[1], rs.at[1], below)
-                elif d == 1:
-                    send(bundle.at[:, hi], from_l.at[j, ch, :, hi], ss.at[2], rs.at[2], above)
-                elif d == 3:
-                    send(bundle.at[:, lo], from_r.at[j, ch, :, lo], ss.at[3], rs.at[3], below)
-
-    def hops(ch):
+    def hand_out(rc, d):
+        ch, (lo, hi, _) = rc // 2, cuts_of(rc)
+        slot = pl.ds(A * (rc % 2), A)
+        for j in range(2):
+            above, below = ends(j)
+            bundle = part.at[j, ch, pl.ds(mod(axes(j)[1] + d, SIDE) * SIDE, SIDE)]
+            ss, rs = r1_s.at[j, rc], r1_r.at[j, rc]
+            if d == 2:
+                send(bundle.at[:, lo], hop.at[j, ch, 0, :, slot], ss.at[0], rs.at[0], above)
+                send(bundle.at[:, hi], hop.at[j, ch, 1, :, slot], ss.at[1], rs.at[1], below)
+            elif d == 1:
+                send(bundle.at[:, hi], from_l.at[j, ch, :, hi], ss.at[2], rs.at[2], above)
+            elif d == 3:
+                send(bundle.at[:, lo], from_r.at[j, ch, :, lo], ss.at[3], rs.at[3], below)
+
+    def down(ch, d):
+        def step(i, carry):
+            j, aa = lax.rem(i, 2), lax.div(i, 2)
+            sh = mod(axes(j)[1] + d, SIDE) * SIDE + aa
+            made = dot(inner[j, ch], wts[j, 2, :, column(j, sh)], 1, 0).astype(BF)
+            part[j, ch, sh] = made.reshape(Q, two, wide)
+            return carry
+
+        lax.fori_loop(0, 2 * SIDE, step, 0)
+
+    def hops(rc):
+        ch, (lo, hi, _) = rc // 2, cuts_of(rc)
+        slot = pl.ds(A * (rc % 2), A)
         for way, (d, cut, target) in enumerate(((1, lo, from_l), (3, hi, from_r))):
             for j in range(2):
                 first = mod(axes(j)[1] + d, SIDE) * SIDE
-                got(hop.at[j, ch, way], r1_s.at[j, ch, way], r1_r.at[j, ch, way])
-
-                def step(aa, carry, j=j, first=first, cut=cut, way=way):
-                    mixed = part[j, ch, first + aa, cut].astype(F32) + hop[j, ch, way, aa].astype(
-                        F32
-                    )
-                    part[j, ch, first + aa, cut] = mixed.astype(BF)
-                    return carry
-
-                lax.fori_loop(0, SIDE, step, 0)
+                here_hop = hop.at[j, ch, way, :, slot]
+                got(here_hop, r1_s.at[j, rc, way], r1_r.at[j, rc, way])
+                mine_part = part.at[j, ch, pl.ds(first, SIDE), cut]
+                mine_part[...] = (mine_part[...].astype(F32) + here_hop[...].astype(F32)).astype(BF)
                 send(
-                    part.at[j, ch, pl.ds(first, SIDE), cut], target.at[j, ch, :, cut],
-                    r2_s.at[j, ch, way], r2_r.at[j, ch, way], ends(j)[way],
+                    mine_part, target.at[j, ch, :, cut],
+                    r2_s.at[j, rc, way], r2_r.at[j, rc, way], ends(j)[way],
                 )
 
-    def columns(ch):
+    def columns(rc):
+        ch, (lo, hi, whole) = rc // 2, cuts_of(rc)
         for j in range(2):
             a, b = axes(j)
-            got(from_l.at[j, ch, :, hi], r1_s.at[j, ch, 2], r1_r.at[j, ch, 2])
-            got(from_r.at[j, ch, :, lo], r1_s.at[j, ch, 3], r1_r.at[j, ch, 3])
-            got(from_l.at[j, ch, :, lo], r2_s.at[j, ch, 0], r2_r.at[j, ch, 0])
-            got(from_r.at[j, ch, :, hi], r2_s.at[j, ch, 1], r2_r.at[j, ch, 1])
+            got(from_l.at[j, ch, :, hi], r1_s.at[j, rc, 2], r1_r.at[j, rc, 2])
+            got(from_r.at[j, ch, :, lo], r1_s.at[j, rc, 3], r1_r.at[j, rc, 3])
+            got(from_l.at[j, ch, :, lo], r2_s.at[j, rc, 0], r2_r.at[j, rc, 0])
+            got(from_r.at[j, ch, :, hi], r2_s.at[j, rc, 1], r2_r.at[j, rc, 1])
 
             def step(i, carry, j=j, a=a, b=b):
                 m = lax.rem(SIDE + 2 - i, SIDE)
                 aa = mod(a + m, SIDE)
                 mixed = (
-                    part[j, ch, b * SIDE + aa].astype(F32)
-                    + from_l[j, ch, aa].astype(F32)
-                    + from_r[j, ch, aa].astype(F32)
+                    part[j, ch, b * SIDE + aa, whole].astype(F32)
+                    + from_l[j, ch, aa, whole].astype(F32)
+                    + from_r[j, ch, aa, whole].astype(F32)
                 )
-                vsum[j, ch, m] = mixed.astype(BF)
+                vsum[j, ch, m, whole] = mixed.astype(BF)
 
                 @pl.when(m > 0)
                 def _():
                     send(
-                        vsum.at[j, ch, m], cross.at[j, ch, m], c_s.at[j, ch, m],
-                        c_r.at[j, ch, m], device(j, aa, b),
+                        vsum.at[j, ch, m, whole], cross.at[j, ch, m, whole], c_s.at[j, rc, m],
+                        c_r.at[j, rc, m], device(j, aa, b),
                     )
 
                 return carry
 
             lax.fori_loop(0, SIDE, step, 0)
 
-    def finish(ch):
+    def finish(rc):
+        ch, (_, _, whole) = rc // 2, cuts_of(rc)
         for j in range(2):
             own = lax.rem(axes(j)[0], 2)
             for m in (1, 3, 2):
-                got(cross.at[j, ch, m], c_s.at[j, ch, m], c_r.at[j, ch, m])
-            final[j, pl.ds(H * (1 - own) + Q * ch, Q)] = (
-                cross[j, ch, 1].astype(F32) + cross[j, ch, 3].astype(F32)
+                got(cross.at[j, ch, m, whole], c_s.at[j, rc, m], c_r.at[j, rc, m])
+            final[j, pl.ds(H * (1 - own) + 2 * A * rc, 2 * A)] = (
+                cross[j, ch, 1, whole].astype(F32) + cross[j, ch, 3, whole].astype(F32)
             ).astype(BF)
-            final[j, pl.ds(H * own + Q * ch, Q)] = (
-                vsum[j, ch, 0].astype(F32) + cross[j, ch, 2].astype(F32)
+            final[j, pl.ds(H * own + 2 * A * rc, 2 * A)] = (
+                vsum[j, ch, 0, whole].astype(F32) + cross[j, ch, 2, whole].astype(F32)
             ).astype(BF)
 
-    accg[...] = jnp.zeros_like(accg)
-    accu[...] = jnp.zeros_like(accu)
-    ssq[...] = jnp.zeros_like(ssq)
-    near(1)
-    for m in range(1, SIDE):
-        got(gains.at[pl.ds(mod(y - m, SIDE) * SIDE, SIDE)], gn_s.at[1, m], gn_r.at[1, m])
-    for j in range(2):
-        for i, w in enumerate((w_gate, w_up, w_down)):
-            pltpu.make_async_copy(w.at[j], wts.at[j, i, pl.ds(0, fh)], wl_r.at[j, i]).wait()
-            got(wts.at[j, i, pl.ds(fh, fh)], w_s.at[j, i], w_r.at[j, i])
-    near(0)
-    multiply_near(1)
-    side(1, True)
-    side(0, False)
-    multiply_near(0)
-    far(1)
-    activate(1)
-    down(1)
-    multiply_side(0)
-    far(0)
-    activate(0)
-    hops(1)
-    down(0)
+        def step(i, carry):
+            combine(2 * A * (rc + 1) - 1 - lax.div(i, 2) + H * lax.rem(i + 1, 2))
+            return carry
+
+        lax.fori_loop(0, 4 * A, step, 0)
 
     def combine(r):
         stacked = jnp.concatenate([final[0, r], final[1, r]], axis=0)
@@ -454,70 +440,84 @@
         got(sib.at[r], cs_s.at[r], cs_r.at[r])
         for u in range(2):
             cut = pl.ds(u * hn, hn)
-
-            @pl.when(s == 0)
-            def _():
-                cont[r, c, cut] = (cont[r, c, cut].astype(F32) + sib[r, cut].astype(F32)).astype(BF)
-
-            @pl.when(s > 0)
-            def _():
+            mixed = cont[r, c, cut].astype(F32) + sib[r, cut].astype(F32)
+            if s:
                 got(zin.at[way, s - 1, cut], q_s.at[way, s - 1, u], q_r.at[way, s - 1, u])
-                cont[r, c, cut] = (
-                    cont[r, c, cut].astype(F32)
-                    + sib[r, cut].astype(F32)
-                    + zin[way, s - 1, cut].astype(F32)
-                ).astype(BF)
-
+                mixed = mixed + zin[way, s - 1, cut].astype(F32)
+            cont[r, c, cut] = mixed.astype(BF)
             send(
                 cont.at[r, c, cut], zin.at[way, s, cut], q_s.at[way, s, u], q_r.at[way, s, u], to
             )
 
-    def place_right(s):
-        return jnp.where(s == 0, Z - 1, H - s)
-
-    def ring_first(s, carry):
-        @pl.when(s < Q)
-        def _():
-            combine(H - 1 - s)
-
-            @pl.when(s < Q - 1)
-            def _():
-                combine(Z - 2 - s)
-
-        pass_on(0, s, place_right(s), z_up)
-
-        @pl.when((s > 0) & (s < Q))
-        def _():
-            pass_on(1, s - 1, Z - 1 - s, z_down)
-
-        return carry
-
-    def ring_last(s, carry):
-        pass_on(1, s - 2, Z - s, z_down)
-
-        @pl.when(s < H)
-        def _():
-            combine(H - 1 - s)
-            pass_on(0, s, H - s, z_up)
-
-        @pl.when(s < H)
-        def _():
-            combine(Z - 1 - s)
-
-        return carry
-
+    def right(s):
+        pass_on(0, s, Z - 1 if s == 0 else H - s, z_up)
+
+    def leftward(s):
+        pass_on(1, s, Z - 2 - s, z_down)
+
+    accg[...] = jnp.zeros_like(accg)
+    accu[...] = jnp.zeros_like(accu)
+    ssq[...] = jnp.zeros_like(ssq)
+    near(1)
+    for m in range(1, SIDE):
+        got(gains.at[pl.ds(mod(y - m, SIDE) * SIDE, SIDE)], gn_s.at[1, m], gn_r.at[1, m])
+
+    def weights_here(kinds):
+        for i in kinds:
+            for j in range(2):
+                w = (w_gate, w_up, w_down)[i]
+                pltpu.make_async_copy(w.at[j], wts.at[j, i, pl.ds(0, fh)], wl_r.at[j, i]).wait()
+                got(wts.at[j, i, pl.ds(fh, fh)], w_s.at[j, i], w_r.at[j, i])
+
+    near(0)
+    weights_here((0, 1, 2))
+    multiply_near(1)
+    side(1, True)
+    side(0, True)
+    multiply_near(0)
+    far(1)
+    activate(1)
+    for d in (2, 1, 3, 0):
+        down(1, d)
+        hand_out(3, d)
+        hand_out(2, d)
+    far(0)
+    activate(0)
+    hops(3)
+    down(0, 2)
+    down(0, 1)
+    hops(2)
+    down(0, 3)
+    for d in (2, 1, 3):
+        hand_out(1, d)
+    columns(3)
+    down(0, 0)
+    for d in (2, 1, 3):
+        hand_out(0, d)
+    columns(2)
+    finish(3)
+    right(0)
+    hops(1)
+    right(1)
+    leftward(0)
+    finish(2)
+    hops(0)
+    right(2)
     columns(1)
+    right(3)
+    leftward(1)
     finish(1)
-    combine(Z - 1)
-    lax.fori_loop(0, 2, ring_first, 0)
-    hops(0)
-    lax.fori_loop(2, Q, ring_first, 0)
     columns(0)
-    lax.fori_loop(Q, Q + 1, ring_first, 0)
+    right(4)
+    leftward(2)
+    right(5)
+    leftward(3)
     finish(0)
-    combine(H + Q - 1)
-    combine(Q - 1)
-    lax.fori_loop(Q + 1, H + 1, ring_last, 0)
+    right(6)
+    leftward(4)
+    right(7)
+    leftward(5)
+    leftward(6)
     got(sib.at[0], cs_s.at[0], cs_r.at[0])
     for u in range(2):
         cut = pl.ds(u * hn, hn)
@@ -566,20 +566,25 @@
         @pl.when(k > 0)
         def _():
             left(piece, a_s.at[j, ch, k], a_r.at[j, ch, k])
-            left(piece, c_s.at[j, ch, k], c_r.at[j, ch, k])
 
         left(piece, b_s.at[j, ch, k, 0], b_r.at[j, ch, k, 0])
         left(piece, b_s.at[j, ch, k, 1], b_r.at[j, ch, k, 1])
         left(piece, f_s.at[j, ch, k], f_r.at[j, ch, k])
-        left(hop.at[j, ch, 0], r1_s.at[j, ch, k], r1_r.at[j, ch, k])
-
-        @pl.when(k < 2)
-        def _():
-            left(hop.at[j, ch, 0], r2_s.at[j, ch, k], r2_r.at[j, ch, k])
-
         return carry
 
     lax.fori_loop(0, 4 * SIDE, left_pieces, 0)
+
+    def left_parts(i, carry):
+        j, rc = lax.rem(i, 2), lax.div(i, 2)
+        for k in range(SIDE):
+            left(hop.at[0, 0, 0, :, pl.ds(0, A)], r1_s.at[j, rc, k], r1_r.at[j, rc, k])
+            if k:
+                left(cross.at[0, 0, 0, pl.ds(0, 2 * A)], c_s.at[j, rc, k], c_r.at[j, rc, k])
+            if k < 2:
+                left(hop.at[0, 0, 0, :, pl.ds(0, A)], r2_s.at[j, rc, k], r2_r.at[j, rc, k])
+        return carry
+
+    lax.fori_loop(0, 8, left_parts, 0)
 
 
 def body(hidden_in, norm_gain, expert_ids, route_weights, w_gate, w_up, w_down):
@@ -621,9 +626,9 @@
         dma((2, 2, SIDE)), dma((2, 2, SIDE)),
         dma((2, 2, SIDE, 2)), dma((2, 2, SIDE, 2)),
         dma((2, 2, SIDE)), dma((2, 2, SIDE)),
-        dma((2, 2, SIDE)), dma((2, 2, SIDE)),
-        dma((2, 2, 2)), dma((2, 2, 2)),
-        dma((2, 2, SIDE)), dma((2, 2, SIDE)),
+        dma((2, 4, SIDE)), dma((2, 4, SIDE)),
+        dma((2, 4, 2)), dma((2, 4, 2)),
+        dma((2, 4, SIDE)), dma((2, 4, SIDE)),
         dma((Z,)), dma((Z,)),
         dma((2, H, 2)), dma((2, H, 2)),
     ]

time: 148 us -> 140 us (0.946)
  Pallas kernels: 142 us -> 135 us
    pallas_call x1, Pallas kernels: 142 us -> 135 us  [body(): pl.pallas_call(functools.partial(kernel, Z, capacity, wide * shards), out...]
where the time goes in v4:
time: 140 us; the launch traced here: 139 us
  Pallas kernels  135 us (96%)
  local copies, waits for them, and re-layouts  4.29 us (3%)
    pallas_call x1, Pallas kernels, body(): pl.pallas_call(functools.partial(kernel, Z, capacity, wide * shards), out...  135 us
    unnamed x3, local copies, waits for them, and re-layouts  4.29 us

profile of v4, /device:TPU:6, one launch (start us, length us, event | category | flops | bytes accessed | tf_op | source)
XLA Modules:
  0.0 139.4 jit_solution(18048486314999767356)
XLA Ops:
  0.0 1.4 %copy.8.ids_in = s32[128,8]{1,0:T(8,128)} copy(s32[128,8]{0,1:T(8,128)} %param.9) | data formatting | bytes 8192 | tf_op args[2]
  1.4 1.4 %copy.9.weights_in = f32[128,8]{1,0:T(8,128)} copy(f32[128,8]{0,1:T(8,128)} %param.10) | data formatting | bytes 8192 | tf_op args[3]
  2.8 135.1 %shard_map.73 = bf16[128,256]{1,0:T(8,128)(2,1)} custom-call(bf16[128,256]{1,0:T(8,128)(2,1)} %hid.1, f32[1,256]{1,0:T(1,128)} %bitcast.1, s32[128,8]{1,0:T(8,128)} %copy.8.ids_in, f32[128,8]{1,0:T(8,128)} %copy.9.weights_in, bf16[2,96,4096]{2,1,0:T(8,128)(2,1)} %w_gate.1, bf16[2,96,4096]{2,1,0:T(8,128)(2,1)} %w_up.1, bf16[2,96,4096]{2,1,0:T(8,128)(2,1)} %w_down.1), custom_call_target="tpu_custom_call" | custom-call | tf_op jit(solution)/shard_map/pallas_call | solution.py:637
  137.9 1.5 %copy.11 = bf16[128,256]{1,0:T(8,128)(2,1)} copy(bf16[128,256]{1,0:T(8,128)(2,1)} %shard_map.73) | data formatting | bytes 131072

commit v5 on v4

--- a/solution.py
+++ b/solution.py
@@ -455,6 +455,68 @@
     def leftward(s):
         pass_on(1, s, Z - 2 - s, z_down)
 
+    def left_start():
+        for m in range(1, SIDE):
+            left(gains.at[0], gn_s.at[0, m], gn_r.at[0, m])
+            left(line, gn_s.at[1, m], gn_r.at[1, m])
+
+        def step(s, carry):
+            for u in range(2):
+                left(tok.at[0, cuts[u]], za_s.at[0, s, u], za_r.at[0, s, u])
+
+                @pl.when(s < H - 1)
+                def _():
+                    left(tok.at[0, cuts[u]], za_s.at[1, s, u], za_r.at[1, s, u])
+
+            left(tok.at[0], sb_s.at[s], sb_r.at[s])
+            left(tok.at[0], sb_s.at[H + s], sb_r.at[H + s])
+            return carry
+
+        lax.fori_loop(0, H, step, 0)
+        for j in range(2):
+            for i, w in enumerate((w_gate, w_up, w_down)):
+                left(w.at[j], w_s.at[j, i], w_r.at[j, i])
+
+    def left_pieces():
+        def step(i, carry):
+            j, ch, k = lax.rem(i, 2), lax.rem(lax.div(i, 2), 2), lax.div(i, 4)
+            piece = gath.at[j, ch, 0]
+
+            @pl.when(k > 0)
+            def _():
+                left(piece, a_s.at[j, ch, k], a_r.at[j, ch, k])
+
+            left(piece, b_s.at[j, ch, k, 0], b_r.at[j, ch, k, 0])
+            left(piece, b_s.at[j, ch, k, 1], b_r.at[j, ch, k, 1])
+            left(piece, f_s.at[j, ch, k], f_r.at[j, ch, k])
+            return carry
+
+        lax.fori_loop(0, 4 * SIDE, step, 0)
+
+    def left_part(rc):
+        for j in range(2):
+            for k in range(SIDE):
+                left(hop.at[0, 0, 0, :, pl.ds(0, A)], r1_s.at[j, rc, k], r1_r.at[j, rc, k])
+                if k:
+                    left(cross.at[0, 0, 0, pl.ds(0, 2 * A)], c_s.at[j, rc, k], c_r.at[j, rc, k])
+                if k < 2:
+                    left(hop.at[0, 0, 0, :, pl.ds(0, A)], r2_s.at[j, rc, k], r2_r.at[j, rc, k])
+
+    def left_ring(s, carry):
+        for u in range(2):
+            cut = pl.ds(u * hn, hn)
+            left(zin.at[0, 0, cut], q_s.at[0, s, u], q_r.at[0, s, u])
+
+            @pl.when(s < H - 1)
+            def _():
+                left(zin.at[1, 0, cut], q_s.at[1, s, u], q_r.at[1, s, u])
+
+        return carry
+
+    def left_cont(r, carry):
+        left(sib.at[0], cs_s.at[r], cs_r.at[r])
+        return carry
+
     accg[...] = jnp.zeros_like(accg)
     accu[...] = jnp.zeros_like(accu)
     ssq[...] = jnp.zeros_like(ssq)
@@ -488,13 +550,15 @@
     down(0, 1)
     hops(2)
     down(0, 3)
+    columns(3)
     for d in (2, 1, 3):
         hand_out(1, d)
-    columns(3)
+    left_start()
     down(0, 0)
+    left_pieces()
+    columns(2)
     for d in (2, 1, 3):
         hand_out(0, d)
-    columns(2)
     finish(3)
     right(0)
     hops(1)
@@ -508,6 +572,9 @@
     leftward(1)
     finish(1)
     columns(0)
+    left_part(3)
+    left_part(2)
+    left_part(1)
     right(4)
     leftward(2)
     right(5)
@@ -530,61 +597,9 @@
             + zin[0, H - 1, cut].astype(F32)
         ).astype(BF)
 
-    for m in range(1, SIDE):
-        left(gains.at[0], gn_s.at[0, m], gn_r.at[0, m])
-        left(line, gn_s.at[1, m], gn_r.at[1, m])
-
-    def left_z(s, carry):
-        for u in range(2):
-            left(tok.at[0, cuts[u]], za_s.at[0, s, u], za_r.at[0, s, u])
-            cut = pl.ds(u * hn, hn)
-            left(zin.at[0, 0, cut], q_s.at[0, s, u], q_r.at[0, s, u])
-
-            @pl.when(s < H - 1)
-            def _():
-                left(tok.at[0, cuts[u]], za_s.at[1, s, u], za_r.at[1, s, u])
-                left(zin.at[1, 0, cut], q_s.at[1, s, u], q_r.at[1, s, u])
-
-        return carry
-
-    lax.fori_loop(0, H, left_z, 0)
-
-    def left_pairs(r, carry):
-        left(tok.at[0], sb_s.at[r], sb_r.at[r])
-        left(sib.at[0], cs_s.at[r], cs_r.at[r])
-        return carry
-
-    lax.fori_loop(0, Z, left_pairs, 0)
-    for j in range(2):
-        for i, w in enumerate((w_gate, w_up, w_down)):
-            left(w.at[j], w_s.at[j, i], w_r.at[j, i])
-
-    def left_pieces(i, carry):
-        j, ch, k = lax.rem(i, 2), lax.rem(lax.div(i, 2), 2), lax.div(i, 4)
-        piece = gath.at[j, ch, 0]
-
-        @pl.when(k > 0)
-        def _():
-            left(piece, a_s.at[j, ch, k], a_r.at[j, ch, k])
-
-        left(piece, b_s.at[j, ch, k, 0], b_r.at[j, ch, k, 0])
-        left(piece, b_s.at[j, ch, k, 1], b_r.at[j, ch, k, 1])
-        left(piece, f_s.at[j, ch, k], f_r.at[j, ch, k])
-        return carry
-
-    lax.fori_loop(0, 4 * SIDE, left_pieces, 0)
-
-    def left_parts(i, carry):
-        j, rc = lax.rem(i, 2), lax.div(i, 2)
-        for k in range(SIDE):
-            left(hop.at[0, 0, 0, :, pl.ds(0, A)], r1_s.at[j, rc, k], r1_r.at[j, rc, k])
-            if k:
-                left(cross.at[0, 0, 0, pl.ds(0, 2 * A)], c_s.at[j, rc, k], c_r.at[j, rc, k])
-            if k < 2:
-                left(hop.at[0, 0, 0, :, pl.ds(0, A)], r2_s.at[j, rc, k], r2_r.at[j, rc, k])
-        return carry
-
-    lax.fori_loop(0, 8, left_parts, 0)
+    left_part(0)
+    lax.fori_loop(0, H, left_ring, 0)
+    lax.fori_loop(0, Z, left_cont, 0)
 
 
 def body(hidden_in, norm_gain, expert_ids, route_weights, w_gate, w_up, w_down):

time: 140 us -> 138 us (0.986)
  Pallas kernels: 135 us -> 132 us
    pallas_call x1, Pallas kernels: 135 us -> 132 us  [body(): pl.pallas_call(functools.partial(kernel, Z, capacity, wide * shards), out...]
where the time goes in v5:
time: 138 us; the launch traced here: 136 us
  Pallas kernels  132 us (96%)
  local copies, waits for them, and re-layouts  4.29 us (3%)
    pallas_call x1, Pallas kernels, body(): pl.pallas_call(functools.partial(kernel, Z, capacity, wide * shards), out...  132 us
    unnamed x3, local copies, waits for them, and re-layouts  4.29 us

profile of v5, /device:TPU:6, one launch (start us, length us, event | category | flops | bytes accessed | tf_op | source)
XLA Modules:
  0.0 136.5 jit_solution(6082846809735090262)
XLA Ops:
  0.0 1.4 %copy.8.ids_in = s32[128,8]{1,0:T(8,128)} copy(s32[128,8]{0,1:T(8,128)} %param.9) | data formatting | bytes 8192 | tf_op args[2]
  1.4 1.4 %copy.9.weights_in = f32[128,8]{1,0:T(8,128)} copy(f32[128,8]{0,1:T(8,128)} %param.10) | data formatting | bytes 8192 | tf_op args[3]
  2.8 132.2 %shard_map.73 = bf16[128,256]{1,0:T(8,128)(2,1)} custom-call(bf16[128,256]{1,0:T(8,128)(2,1)} %hid.1, f32[1,256]{1,0:T(1,128)} %bitcast.1, s32[128,8]{1,0:T(8,128)} %copy.8.ids_in, f32[128,8]{1,0:T(8,128)} %copy.9.weights_in, bf16[2,96,4096]{2,1,0:T(8,128)(2,1)} %w_gate.1, bf16[2,96,4096]{2,1,0:T(8,128)(2,1)} %w_up.1, bf16[2,96,4096]{2,1,0:T(8,128)(2,1)} %w_down.1), custom_call_target="tpu_custom_call" | custom-call | tf_op jit(solution)/shard_map/pallas_call | solution.py:652
  135.0 1.5 %copy.11 = bf16[128,256]{1,0:T(8,128)(2,1)} copy(bf16[128,256]{1,0:T(8,128)(2,1)} %shard_map.73) | data formatting | bytes 131072

commit v6 on v5

--- a/solution.py
+++ b/solution.py
@@ -553,17 +553,17 @@
     columns(3)
     for d in (2, 1, 3):
         hand_out(1, d)
-    left_start()
-    down(0, 0)
-    left_pieces()
     columns(2)
     for d in (2, 1, 3):
         hand_out(0, d)
     finish(3)
     right(0)
+    down(0, 0)
     hops(1)
+    left_start()
     right(1)
     leftward(0)
+    left_pieces()
     finish(2)
     hops(0)
     right(2)

time: 138 us -> 137 us (level)
  no operation moved by 1% of the time
where the time goes in v6:
time: 137 us; the launch traced here: 136 us
  Pallas kernels  132 us (96%)
  local copies, waits for them, and re-layouts  4.29 us (3%)
    pallas_call x1, Pallas kernels, body(): pl.pallas_call(functools.partial(kernel, Z, capacity, wide * shards), out...  132 us
    unnamed x3, local copies, waits for them, and re-layouts  4.29 us

profile of v6, /device:TPU:6, one launch (start us, length us, event | category | flops | bytes accessed | tf_op | source)
XLA Modules:
  0.0 136.2 jit_solution(9626527344203365795)
XLA Ops:
  0.0 1.4 %copy.8.ids_in = s32[128,8]{1,0:T(8,128)} copy(s32[128,8]{0,1:T(8,128)} %param.9) | data formatting | bytes 8192 | tf_op args[2]
  1.4 1.4 %copy.9.weights_in = f32[128,8]{1,0:T(8,128)} copy(f32[128,8]{0,1:T(8,128)} %param.10) | data formatting | bytes 8192 | tf_op args[3]
  2.8 131.9 %shard_map.73 = bf16[128,256]{1,0:T(8,128)(2,1)} custom-call(bf16[128,256]{1,0:T(8,128)(2,1)} %hid.1, f32[1,256]{1,0:T(1,128)} %bitcast.1, s32[128,8]{1,0:T(8,128)} %copy.8.ids_in, f32[128,8]{1,0:T(8,128)} %copy.9.weights_in, bf16[2,96,4096]{2,1,0:T(8,128)(2,1)} %w_gate.1, bf16[2,96,4096]{2,1,0:T(8,128)(2,1)} %w_up.1, bf16[2,96,4096]{2,1,0:T(8,128)(2,1)} %w_down.1), custom_call_target="tpu_custom_call" | custom-call | tf_op jit(solution)/shard_map/pallas_call | solution.py:652
  134.7 1.5 %copy.11 = bf16[128,256]{1,0:T(8,128)(2,1)} copy(bf16[128,256]{1,0:T(8,128)(2,1)} %shard_map.73) | data formatting | bytes 131072
